TPU v7x, 32 devices: a whole 2x2x4 slice. The times are simulated.
32 devices in a mesh: seq: 8 (over z, x), batch: 4 (over y, core).
Axes of the slice: x: 2, y: 2, z: 4, core: 2. Of those that a mesh axis runs over, the one named last changes fastest.
Arguments:
- inputs: bfloat16 [32768, 768], P(('batch', 'seq')), parts along dimension 0, may hold values from -6 to 6
- token_rates: float32 [32768], P(('batch', 'seq')), parts along dimension 0, may hold values from 0.1 to 1
- proj_query: bfloat16 [768, 256], replicated, may hold values from -0.21875 to 0.21875
- proj_key: bfloat16 [768, 256], replicated, may hold values from -0.21875 to 0.21875
- proj_value: bfloat16 [768, 256], replicated, may hold values from -0.21875 to 0.21875
- proj_output: bfloat16 [256, 768], replicated, may hold values from -0.375 to 0.375
- fast_in: float32 [256, 512], replicated, may hold values from -0.375 to 0.375
- fast_up: float32 [256, 512], replicated, may hold values from -0.375 to 0.375
- fast_out: float32 [512, 256], replicated, may hold values from -0.25 to 0.25
- cotangent: bfloat16 [32768, 768], P(('batch', 'seq')), parts along dimension 0, may hold values from -6 to 6
Outputs:
- back_inputs: bfloat16 [32768, 768], P(('batch', 'seq')), parts along dimension 0
- back_rate: float32 [32768], P(('batch', 'seq')), parts along dimension 0
- grad_in: float32 [1024, 512], P('batch'), parts along dimension 0
- grad_up: float32 [1024, 512], P('batch'), parts along dimension 0
- grad_out: float32 [2048, 256], P('batch'), parts along dimension 0
- grad_query: float32 [768, 1024], P('seq', 'batch'), parts along dimension 1
- grad_key: float32 [768, 1024], P('seq', 'batch'), parts along dimension 1
- grad_value: float32 [768, 1024], P('seq', 'batch'), parts along dimension 1
- grad_output: float32 [1024, 768], P('batch', 'seq'), parts along dimension 0
There are 4 independent parts, one for each index of `batch`. A program takes and returns all parts, laid end to end along the dimension named above; an argument that names none is the same for every part. Nothing has to cross between parts.
All inputs are finite; a program needn't handle non-finite values.
Results may differ from a plain program's by a relative error of at most 0.029.
Values may be sent and summed in bfloat16 or wider, within the bound.
A program may use at most 128 MiB of HBM per device.

v0:
```python
import jax
import jax.numpy as jnp
from jax import lax
from jax.sharding import PartitionSpec as P

NS_STEPS = 5


def rounded(value):
    return value.astype(jnp.bfloat16)


def product(left, right):
    return jnp.dot(left, right, preferred_element_type=jnp.float32)


def token_sum(left, right):
    return lax.dot_general(
        left, right, (((0,), (0,)), ((), ())), preferred_element_type=jnp.float32
    )


def times_transpose(left, right):
    return lax.dot_general(
        left, right, (((1,), (1,)), ((), ())), preferred_element_type=jnp.float32
    )


def silu_parts(pre_act):
    sigma_val = jax.nn.sigmoid(pre_act)
    activation = pre_act * sigma_val
    slope_val = sigma_val * (1.0 + pre_act * (1.0 - sigma_val))
    curvature = sigma_val * (1.0 - sigma_val) * (2.0 + pre_act * (1.0 - 2.0 * sigma_val))
    return (activation, slope_val, curvature)


def orthogonalize(matrix):
    highest = lax.Precision.HIGHEST
    current = matrix / (jnp.sqrt(jnp.sum(matrix * matrix)) + 1e-07)
    for sweep in range(NS_STEPS):
        gramian = jnp.dot(current, current.T, precision=highest)
        polynom = -4.775 * gramian + 2.0315 * jnp.dot(gramian, gramian, precision=highest)
        current = 3.4445 * current + jnp.dot(polynom, current, precision=highest)
    return current


def project(inputs, proj_query, proj_key, proj_value):
    return (
        rounded(product(inputs, proj_query)),
        rounded(product(inputs, proj_key)),
        rounded(product(inputs, proj_value)),
    )


def update_section(key_rows, value_rows, token_rates, fast_in, fast_up, fast_out):
    w_in, w_up, w_out = (rounded(fast_in), rounded(fast_up), rounded(fast_out))
    scaled = rounded(token_rates[:, None] * value_rows.astype(jnp.float32))
    pre_in = product(key_rows, w_in)
    pre_up = product(key_rows, w_up)
    activation, slope_val, curvature = silu_parts(pre_in)
    hidden = rounded(activation * pre_up)
    upstream = times_transpose(scaled, w_out)
    grad_in_rows = rounded(upstream * pre_up * slope_val)
    grad_up_rows = rounded(upstream * activation)
    partial_value = jnp.stack(
        [
            token_sum(key_rows, grad_in_rows),
            token_sum(key_rows, grad_up_rows),
            token_sum(scaled, hidden),
        ]
    )
    saved = (
        w_in,
        w_up,
        w_out,
        scaled,
        pre_in,
        pre_up,
        hidden,
        upstream,
        grad_in_rows,
        grad_up_rows,
    )
    return (partial_value, saved)


def query_section(query_rows, cotangent, proj_output, new_in, new_up, new_out):
    n_in, n_up, n_out = (rounded(new_in), rounded(new_up), rounded(new_out))
    pre_p = product(query_rows, n_in)
    pre_r = product(query_rows, n_up)
    activation_q, slope_q, unused_curve = silu_parts(pre_p)
    hidden_q = rounded(activation_q * pre_r)
    output_rows = rounded(product(hidden_q, n_out))
    back_output = rounded(times_transpose(cotangent, proj_output))
    back_hidden = times_transpose(back_output, n_out)
    back_p = rounded(back_hidden * pre_r * slope_q)
    back_r = rounded(back_hidden * activation_q)
    partial_value = jnp.stack(
        [
            token_sum(query_rows, back_p),
            token_sum(query_rows, back_r),
            token_sum(back_output, hidden_q),
        ]
    )
    query_grad = rounded(times_transpose(back_p, n_in) + times_transpose(back_r, n_up))
    return (partial_value, query_grad, output_rows)


def update_backward(saved, key_rows, value_rows, token_rates, back_totals):
    w_in, w_up, w_out, scaled, pre_in, pre_up, hidden, upstream, grad_in_rows, grad_up_rows = saved
    activation, slope_val, curvature = silu_parts(pre_in)
    b_in = rounded(back_totals[0])
    b_up = rounded(back_totals[1])
    b_out = rounded(back_totals[2])
    press_in = product(key_rows, b_in)
    press_up = product(key_rows, b_up)
    back_hid = product(scaled, b_out)
    back_upstream = rounded(press_in * pre_up * slope_val + press_up * activation)
    back_pre_up = rounded(press_in * upstream * slope_val + back_hid * activation)
    back_pre_in = rounded(
        press_in * upstream * pre_up * curvature
        + press_up * upstream * slope_val
        + back_hid * pre_up * slope_val
    )
    back_scaled = times_transpose(hidden, b_out) + product(back_upstream, w_out)
    back_rate = jnp.sum(back_scaled * value_rows.astype(jnp.float32), axis=1)
    contrib = (
        token_sum(key_rows, back_pre_in),
        token_sum(key_rows, back_pre_up),
        token_sum(back_upstream, scaled),
    )
    key_sum = times_transpose(grad_in_rows, b_in) + times_transpose(grad_up_rows, b_up)
    key_sum = key_sum + times_transpose(back_pre_in, w_in) + times_transpose(back_pre_up, w_up)
    key_grad = rounded(key_sum)
    value_grad = rounded(token_rates[:, None] * back_scaled)
    return (contrib, key_grad, value_grad, back_rate)


def input_back(query_grad, key_grad, value_grad, proj_query, proj_key, proj_value):
    total = times_transpose(query_grad, proj_query) + times_transpose(key_grad, proj_key)
    return rounded(total + times_transpose(value_grad, proj_value))


def body(
    inputs,
    token_rates,
    proj_query,
    proj_key,
    proj_value,
    proj_output,
    fast_in,
    fast_up,
    fast_out,
    cotangent,
):
    query_rows, key_rows, value_rows = project(inputs, proj_query, proj_key, proj_value)
    partial_value, saved = update_section(
        key_rows, value_rows, token_rates, fast_in, fast_up, fast_out
    )
    totals = lax.psum(partial_value, "seq")
    ortho, ns_back = jax.vjp(jax.vmap(orthogonalize), totals)
    new_in = fast_in + ortho[0]
    new_up = fast_up + ortho[1]
    new_out = fast_out + ortho[2].T
    adjoint_part, query_grad, output_rows = query_section(
        query_rows, cotangent, proj_output, new_in, new_up, new_out
    )
    adjoint = lax.psum(adjoint_part, "seq")
    back_totals = ns_back(adjoint)[0]
    contrib, key_grad, value_grad, back_rate = update_backward(
        saved, key_rows, value_rows, token_rates, back_totals
    )
    summed = lax.psum((contrib[0], contrib[1], contrib[2]), "seq")
    grad_in = adjoint[0] + summed[0]
    grad_up = adjoint[1] + summed[1]
    grad_out = adjoint[2].T + summed[2]
    back_inputs = input_back(query_grad, key_grad, value_grad, proj_query, proj_key, proj_value)
    stacked = jnp.stack(
        [
            token_sum(inputs, query_grad),
            token_sum(inputs, key_grad),
            token_sum(inputs, value_grad),
            token_sum(cotangent, output_rows),
        ]
    )
    shards = lax.psum_scatter(stacked, "seq", scatter_dimension=1, tiled=True)
    grad_query = shards[0]
    grad_key = shards[1]
    grad_value = shards[2]
    grad_output = shards[3].T
    return (
        back_inputs,
        back_rate,
        grad_in,
        grad_up,
        grad_out,
        grad_query,
        grad_key,
        grad_value,
        grad_output,
    )


def solution(mesh):
    in_specs = (
        P(("batch", "seq"), None),
        P(("batch", "seq")),
        P(),
        P(),
        P(),
        P(),
        P(),
        P(),
        P(),
        P(("batch", "seq"), None),
    )
    out_specs = (
        P(("batch", "seq"), None),
        P(("batch", "seq")),
        P("batch", None),
        P("batch", None),
        P("batch", None),
        P("seq", "batch"),
        P("seq", "batch"),
        P("seq", "batch"),
        P("batch", "seq"),
    )
    return jax.shard_map(body, mesh=mesh, in_specs=in_specs, out_specs=out_specs, check_vma=False)
```

profile of v0, /device:TPU:0, one launch (start us, length us, event | category | flops | bytes accessed | tf_op | source)
XLA Modules:
  0.0 496.2 jit_solution(18164545563299364027)
XLA Ops:
  14.1 2.7 multiply_convert_fusion.5
  24.2 88.0 %all-reduce.6.cloned.1.call-done = f32[3,256,512]{2,1,0:T(8,128)} async-done(((f32[3,256,512]{2,1,0:T(8,128)}), f32[3,256,512]{2,1,0:T(8,128)}) %all-reduce.6.cloned.1.call-update) | async-done | bytes 1572880 | tf_op jit(solution)/shard_map/psum | solution.py:160
  112.3 1.8 multiply_reduce_fusion.1
  114.2 1.8 fusion.89
  117.8 1.8 multiply_add_fusion.4
  119.7 1.7 fusion.90
  131.3 1.7 fusion.92
  136.4 1.7 fusion.93
  148.4 1.8 fusion.96
  153.0 4.0 convolution_bitcast_fusion
  157.0 80.0 %all-reduce.8.cloned.1.call-done = f32[3,256,512]{2,1,0:T(8,128)} async-done(((f32[3,256,512]{2,1,0:T(8,128)}), f32[3,256,512]{2,1,0:T(8,128)}) %all-reduce.8.cloned.1.call-update) | async-done | bytes 1572880 | tf_op jit(solution)/shard_map/psum | solution.py:168
  237.0 3.6 fusion.99
  246.7 1.8 add_add_fusion.5
  248.5 2.0 fusion.101
  250.6 1.6 fusion.102
  256.2 1.8 add_add_fusion.4
  259.6 1.6 fusion.105
  261.3 1.6 fusion.31
  265.5 1.8 add_add_fusion.3
  269.0 1.6 fusion.108
  274.6 2.1 add_add_fusion.2
  278.4 1.8 fusion.88
  282.6 1.6 fusion.87
  284.3 2.3 multiply_reduce_fusion
  292.9 2.6 add_convert_fusion.1
  305.0 1.9 pad_maximum_fusion
  306.9 4.9 copy.58
  316.0 1.8 add_convert_fusion
  317.7 163.1 %all-reduce.10.cloned.1.call-done = (f32[256,512]{1,0:T(8,128)}, f32[256,512]{1,0:T(8,128)}, f32[512,256]{0,1:T(8,128)}, f32[4,768,256]{2,0,1:T(4,128)}) async-done(((f32[256,512]{1,0:T(8,128)}, f32[256,512]{1,0:T(8,128)}, f32[512,256]{0,1:T(8,128)}, f32[4,768,256]{2,0,1:T(4,128)}), (f32[256,512]{1,0:T(8,128)}, f32[256,512]{1,0:T(8,128)}, f32[512,256]{0,1:T(8,128)}, ...) | async-done | bytes 4718608 | tf_op jit(solution)/shard_map/psum | solution.py:173
  480.8 1.9 fusion.39
  482.7 2.0 copy.59
  484.8 2.0 constant_dynamic-slice_fusion.3
  (241 shorter events, 87.8 us)
Async XLA Ops:
  7.2 3.0 copy-start.35
  7.2 105.1 %all-reduce.6.cloned.1.call-start = ((), (), s32[]{:S(2)}) async-start(), calls=%async_computation | async-start | bytes 3145728 | tf_op jit(solution)/shard_map/psum | solution.py:160
  10.2 7.0 %copy-start.7 = (bf16[1024,256]{1,0:T(8,128)(2,1)}, bf16[1024,256]{1,0:T(8,128)(2,1)S(1)}, u32[]{:S(2)}) copy-start(bf16[1024,256]{1,0:T(8,128)(2,1)S(1)} %convolution_convert_fusion.3) | copy-start | bytes 1572868
  11.4 1.9 copy-start.58
  12.7 4.1 copy-start.60
  14.1 4.0 copy-start.21
  20.1 216.9 %all-reduce.8.cloned.1.call-start = ((), (), s32[]{:S(2)}) async-start(), calls=%async_computation.1 | async-start | bytes 3145728 | tf_op jit(solution)/shard_map/psum | solution.py:168
  112.3 1.9 copy-start.19
  117.8 1.8 copy-start.54
  119.7 2.6 copy-start.5
  121.3 3.4 copy-start.11
  131.3 3.5 copy-start.1
  136.4 2.6 copy-start.3
  138.1 2.6 copy-start.17
  148.3 332.5 %all-reduce.10.cloned.1.call-start = ((), (), s32[]{:S(2)}) async-start(), calls=%async_computation.2 | async-start | bytes 9437184 | tf_op jit(solution)/shard_map/psum | solution.py:173
  148.4 1.8 copy-start.52
  148.4 1.8 copy-start.70
  237.0 3.6 copy-start.18
  246.7 1.8 copy-start.32
  248.5 2.0 copy-start.2
  256.2 1.8 copy-start.30
  265.5 1.8 copy-start.28
  274.6 2.1 copy-start.55
  278.4 1.8 copy-start.24
  288.9 3.0 copy-start.81
  290.0 2.1 copy-start.61
  291.2 1.7 copy-start.59
  311.7 1.9 copy-start.43
  311.7 1.9 copy-start.75
  316.0 164.8 %copy-start.10 = (f32[3,256,512]{2,1,0:T(8,128)S(1)}, f32[3,256,512]{2,1,0:T(8,128)}, u32[]{:S(2)}) copy-start(f32[3,256,512]{2,1,0:T(8,128)} %all-reduce.8.cloned.1.call-done) | copy-start | bytes 4718596
  484.8 3.3 copy-start.72
  484.8 3.3 copy-start.73
  (53 other events, 69.0 us)
Sparse Core Ops, SparseCore 0:
  20.2 92.0 all-reduce.5
  148.4 88.5 all-reduce.7
  311.9 168.8 all-reduce.9
where the time goes:
time: 501 us; the launch traced here: 496 us
  waiting for transfers between devices  331 us (66%)
  matrix products  107 us (21%)
  local copies, waits for them, and re-layouts  31.8 us (6%)
  between operations  16 us (3%)
  other arithmetic  10.1 us (2%)
    psum x1, waiting for transfers between devices, body(): summed = lax.psum((contrib[0], contrib[1], contrib[2]), 'seq')  163 us
    psum x1, waiting for transfers between devices, body(): totals = lax.psum(partial_value, 'seq')  88 us
    psum x1, waiting for transfers between devices, body(): adjoint = lax.psum(adjoint_part, 'seq')  80 us
    dot_general x15, matrix products, orthogonalize(): current = 3.4445 * current + jnp.dot(polynom, current, precision=highest)  26.7 us
    dot_general x15, matrix products, orthogonalize(): gramian = jnp.dot(current, current.T, precision=highest)  26 us
    unnamed x168, local copies, waits for them, and re-layouts  24.3 us
    dot_general x15, matrix products, orthogonalize(): jnp.dot(gramian, gramian, precision=highest)  17.6 us
    dot_general x13, matrix products, token_sum(): lax.dot_general(left, right, (((0,), (0,)), ((), ())), preferred_element_...  13.1 us
  transfers between devices with their start and end apart: 3, of which 3 were waited for; matrix products, arithmetic and copies ran while one was open for 3% of the time, Pallas kernels for 0%

commit v1 on v0

v1 whole, which is shorter than its diff:
```python
import functools

import jax
import jax.numpy as jnp
from jax import lax
from jax.experimental import pallas as pl
from jax.experimental.pallas import tpu as pltpu
from jax.sharding import PartitionSpec as P

NS_STEPS = 5
C1, C3, C5 = 3.4445, -4.775, 2.0315
EPS = 1e-07
MESH = pl.DeviceIdType.MESH
VMEM_LIMIT = 60 * 1024 * 1024
PASSES_FWD = 3
PASSES_BWD = 3


def rounded(value):
    return value.astype(jnp.bfloat16)


def product(left, right):
    return jnp.dot(left, right, preferred_element_type=jnp.float32)


def token_sum(left, right):
    return lax.dot_general(
        left, right, (((0,), (0,)), ((), ())), preferred_element_type=jnp.float32
    )


def times_transpose(left, right):
    return lax.dot_general(
        left, right, (((1,), (1,)), ((), ())), preferred_element_type=jnp.float32
    )


def silu_parts(pre_act):
    sigma_val = jax.nn.sigmoid(pre_act)
    activation = pre_act * sigma_val
    slope_val = sigma_val * (1.0 + pre_act * (1.0 - sigma_val))
    curvature = sigma_val * (1.0 - sigma_val) * (2.0 + pre_act * (1.0 - 2.0 * sigma_val))
    return (activation, slope_val, curvature)


def split(value):
    high = rounded(value)
    return (high, rounded(value - high.astype(jnp.float32)))


def dot_split(left, right, passes, dot):
    if passes == 1:
        return dot(left[0], right[0])
    return dot(left[0], right[0]) + (dot(left[0], right[1]) + dot(left[1], right[0]))


def ns_forward(totals, xs, grams, polys, count, passes):
    norms = []
    for m in range(count):
        norm = jnp.sqrt(jnp.sum(totals[m] * totals[m]))
        norms.append(norm)
        xs[0, m] = totals[m] / (norm + EPS)

    def step(k, carry):
        for m in range(count):
            current = xs[k, m]
            parts = split(current)
            gram = dot_split(parts, parts, passes, times_transpose)
            gparts = split(gram)
            poly = C3 * gram + C5 * dot_split(gparts, gparts, passes, product)
            if grams is not None:
                grams[k, m] = gram
                polys[k, m] = poly
            xs[k + 1, m] = C1 * current + dot_split(split(poly), parts, passes, product)
        return carry

    lax.fori_loop(0, NS_STEPS, step, 0)
    return norms


def ns_backward(totals, norms, xs, grams, polys, grads, count, passes):
    def step(i, carry):
        k = NS_STEPS - 1 - i
        for m in range(count):
            grad = grads[m]
            gparts = split(grad)
            xparts = split(xs[k, m])
            dpoly = dot_split(gparts, xparts, passes, times_transpose)
            sym = dpoly + dpoly.T
            twist = dot_split(split(sym), split(grams[k, m]), passes, product)
            weight = C3 * sym + C5 * (twist + twist.T)
            grads[m] = (
                C1 * grad
                + dot_split(split(polys[k, m]), gparts, passes, product)
                + dot_split(split(weight), xparts, passes, product)
            )
        return carry

    lax.fori_loop(0, NS_STEPS, step, 0)
    out = []
    for m in range(count):
        shifted = norms[m] + EPS
        dot_all = jnp.sum(grads[m] * totals[m])
        out.append(grads[m] / shifted - totals[m] * (dot_all / (norms[m] * shifted * shifted)))
    return out


def greet(n):
    me = lax.axis_index("seq")
    barrier = pltpu.get_barrier_semaphore()
    for d in range(1, n):
        pl.semaphore_signal(
            barrier, inc=1, device_id={"seq": lax.rem(me + d, n)}, device_id_type=MESH
        )
    pl.semaphore_wait(barrier, n - 1)


def start_scatter(n, src, landed, send, recv):
    me = lax.axis_index("seq")
    copies = []
    for d in range(1, n):
        peer = lax.rem(me + d, n)
        copy = pltpu.make_async_remote_copy(
            src_ref=src.at[peer],
            dst_ref=landed.at[d - 1],
            send_sem=send.at[d - 1],
            recv_sem=recv.at[d - 1],
            device_id={"seq": peer},
            device_id_type=MESH,
        )
        copy.start()
        copies.append(copy)
    return copies


def finish_scatter(src, landed, copies):
    total = src[lax.axis_index("seq")].astype(jnp.float32)
    for i, copy in enumerate(copies):
        copy.wait()
        total = total + landed[i].astype(jnp.float32)
    return total


def start_gather(n, mine, gathered, send, recv):
    me = lax.axis_index("seq")
    copies = []
    for d in range(1, n):
        copy = pltpu.make_async_remote_copy(
            src_ref=mine,
            dst_ref=gathered.at[d - 1],
            send_sem=send.at[d - 1],
            recv_sem=recv.at[d - 1],
            device_id={"seq": lax.rem(me + d, n)},
            device_id_type=MESH,
        )
        copy.start()
        copies.append(copy)
    return copies


def finish_gather(n, mine, gathered, copies, full):
    me = lax.axis_index("seq")
    rows = mine.shape[0]
    full[pl.ds(pl.multiple_of(me * rows, rows), rows), :] = mine[...].astype(jnp.float32)
    for d in range(1, n):
        copies[d - 1].wait()
        owner = lax.rem(me - d + n, n)
        full[pl.ds(pl.multiple_of(owner * rows, rows), rows), :] = gathered[d - 1].astype(
            jnp.float32
        )


def forward_kernel(
    n, count, part, fast_in, fast_up, fast_out, n_in, n_up, n_out, total_out,
    landed, mine, gathered, xs, s1, r1, s2, r2,
):
    greet(n)
    copies = start_scatter(n, part, landed, s1, r1)
    mine[...] = rounded(finish_scatter(part, landed, copies))
    copies = start_gather(n, mine, gathered, s2, r2)
    finish_gather(n, mine, gathered, copies, total_out)
    h = total_out.shape[0] // count
    totals = [total_out[m * h : (m + 1) * h, :] for m in range(count)]
    ns_forward(totals, xs, None, None, count, PASSES_FWD)
    n_in[...] = rounded(fast_in[...] + xs[NS_STEPS, 0])
    n_up[...] = rounded(fast_up[...] + xs[NS_STEPS, 1])
    n_out[...] = rounded(fast_out[...] + xs[NS_STEPS, 2].T)


def backward_kernel(
    n, count, part, rows_part, total_ref, adjoint_out, back_out, rows_out,
    landed, mine, gathered, landed_rows, xs, grams, polys, grads, s1, r1, s2, r2, s3, r3,
):
    greet(n)
    copies = start_scatter(n, part, landed, s1, r1)
    h = total_ref.shape[0] // count
    totals = [total_ref[m * h : (m + 1) * h, :] for m in range(count)]
    norms = ns_forward(totals, xs, grams, polys, count, PASSES_FWD)
    mine[...] = rounded(finish_scatter(part, landed, copies))
    copies = start_gather(n, mine, gathered, s2, r2)
    finish_gather(n, mine, gathered, copies, adjoint_out)
    row_copies = start_scatter(n, rows_part, landed_rows, s3, r3)
    for m in range(count):
        grads[m] = adjoint_out[m * h : (m + 1) * h, :]
    result = ns_backward(totals, norms, xs, grams, polys, grads, count, PASSES_BWD)
    for m in range(count):
        back_out[m * h : (m + 1) * h, :] = rounded(result[m])
    rows_out[...] = finish_scatter(rows_part, landed_rows, row_copies)


def final_kernel(
    n, part, rows_part, sum_out, rows_out,
    landed, mine, gathered, landed_rows, s1, r1, s2, r2, s3, r3,
):
    greet(n)
    copies = start_scatter(n, part, landed, s1, r1)
    row_copies = start_scatter(n, rows_part, landed_rows, s3, r3)
    mine[...] = rounded(finish_scatter(part, landed, copies))
    copies = start_gather(n, mine, gathered, s2, r2)
    rows_out[...] = finish_scatter(rows_part, landed_rows, row_copies)
    finish_gather(n, mine, gathered, copies, sum_out)


def call(kernel, identity, outs, scratch, *operands):
    vmem = pl.BlockSpec(memory_space=pltpu.VMEM)
    return pl.pallas_call(
        kernel,
        out_shape=[jax.ShapeDtypeStruct(s, d) for s, d in outs],
        in_specs=[vmem] * len(operands),
        out_specs=[vmem] * len(outs),
        scratch_shapes=scratch,
        compiler_params=pltpu.CompilerParams(
            collective_id=identity, has_side_effects=True, vmem_limit_bytes=VMEM_LIMIT
        ),
    )(*operands)


def sems(n, count):
    return [pltpu.SemaphoreType.DMA((n - 1,)) for _ in range(count)]


def body(
    n,
    inputs,
    token_rates,
    proj_query,
    proj_key,
    proj_value,
    proj_output,
    fast_in,
    fast_up,
    fast_out,
    cotangent,
):
    bf16, f32 = jnp.bfloat16, jnp.float32
    h, f = fast_in.shape
    width = inputs.shape[1]
    count = 3
    block = (count * h // n, f)
    row_block = (width // n, 2 * h)

    query_rows = rounded(product(inputs, proj_query))
    key_rows = rounded(product(inputs, proj_key))
    value_rows = rounded(product(inputs, proj_value))
    w_in, w_up, w_out = (rounded(fast_in), rounded(fast_up), rounded(fast_out))
    scaled = rounded(token_rates[:, None] * value_rows.astype(f32))
    pre_in = product(key_rows, w_in)
    pre_up = product(key_rows, w_up)
    activation, slope_val, curvature = silu_parts(pre_in)
    hidden = rounded(activation * pre_up)
    upstream = times_transpose(scaled, w_out)
    grad_in_rows = rounded(upstream * pre_up * slope_val)
    grad_up_rows = rounded(upstream * activation)

    def stacked(*terms):
        return jnp.concatenate([rounded(t) for t in terms]).reshape((n,) + block)

    def row_stacked(left, right):
        return jnp.concatenate([rounded(left), rounded(right)], axis=1).reshape((n,) + row_block)

    part = stacked(
        token_sum(key_rows, grad_in_rows),
        token_sum(key_rows, grad_up_rows),
        token_sum(scaled, hidden),
    )
    exchange = [
        pltpu.VMEM((n - 1,) + block, bf16),
        pltpu.VMEM(block, bf16),
        pltpu.VMEM((n - 1,) + block, bf16),
    ]
    n_in, n_up, n_out, totals = call(
        functools.partial(forward_kernel, n, count),
        0,
        [((h, f), bf16), ((h, f), bf16), ((f, h), bf16), ((count * h, f), f32)],
        exchange + [pltpu.VMEM((NS_STEPS + 1, count, h, f), f32)] + sems(n, 4),
        part, fast_in, fast_up, fast_out,
    )

    pre_p = product(query_rows, n_in)
    pre_r = product(query_rows, n_up)
    activation_q, slope_q, _ = silu_parts(pre_p)
    hidden_q = rounded(activation_q * pre_r)
    output_rows = rounded(product(hidden_q, n_out))
    back_output = rounded(times_transpose(cotangent, proj_output))
    back_hidden = times_transpose(back_output, n_out)
    back_p = rounded(back_hidden * pre_r * slope_q)
    back_r = rounded(back_hidden * activation_q)
    query_grad = rounded(times_transpose(back_p, n_in) + times_transpose(back_r, n_up))
    part = stacked(
        token_sum(query_rows, back_p),
        token_sum(query_rows, back_r),
        token_sum(back_output, hidden_q),
    )
    rows_part = row_stacked(token_sum(inputs, query_grad), token_sum(cotangent, output_rows))
    row_scratch = [pltpu.VMEM((n - 1,) + row_block, bf16)]
    adjoint, back_totals, rows_sum = call(
        functools.partial(backward_kernel, n, count),
        1,
        [((count * h, f), f32), ((count * h, f), bf16), (row_block, f32)],
        exchange
        + row_scratch
        + [
            pltpu.VMEM((NS_STEPS + 1, count, h, f), f32),
            pltpu.VMEM((NS_STEPS, count, h, h), f32),
            pltpu.VMEM((NS_STEPS, count, h, h), f32),
            pltpu.VMEM((count, h, f), f32),
        ]
        + sems(n, 6),
        part, rows_part, totals,
    )
    grad_query = rows_sum[:, :h]
    grad_output = rows_sum[:, h:].T

    b_in, b_up, b_out = (back_totals[m * h : (m + 1) * h] for m in range(count))
    press_in = product(key_rows, b_in)
    press_up = product(key_rows, b_up)
    back_hid = product(scaled, b_out)
    back_upstream = rounded(press_in * pre_up * slope_val + press_up * activation)
    back_pre_up = rounded(press_in * upstream * slope_val + back_hid * activation)
    back_pre_in = rounded(
        press_in * upstream * pre_up * curvature
        + press_up * upstream * slope_val
        + back_hid * pre_up * slope_val
    )
    back_scaled = times_transpose(hidden, b_out) + product(back_upstream, w_out)
    back_rate = jnp.sum(back_scaled * value_rows.astype(f32), axis=1)
    key_sum = times_transpose(grad_in_rows, b_in) + times_transpose(grad_up_rows, b_up)
    key_sum = key_sum + times_transpose(back_pre_in, w_in) + times_transpose(back_pre_up, w_up)
    key_grad = rounded(key_sum)
    value_grad = rounded(token_rates[:, None] * back_scaled)
    part = stacked(
        token_sum(key_rows, back_pre_in),
        token_sum(key_rows, back_pre_up),
        token_sum(scaled, back_upstream),
    )
    rows_part = row_stacked(token_sum(inputs, key_grad), token_sum(inputs, value_grad))
    summed, rows_sum = call(
        functools.partial(final_kernel, n),
        2,
        [((count * h, f), f32), (row_block, f32)],
        exchange + row_scratch + sems(n, 6),
        part, rows_part,
    )
    grad_key = rows_sum[:, :h]
    grad_value = rows_sum[:, h:]
    both = adjoint + summed
    grad_in = both[:h]
    grad_up = both[h : 2 * h]
    grad_out = both[2 * h :].T
    total = times_transpose(query_grad, proj_query) + times_transpose(key_grad, proj_key)
    back_inputs = rounded(total + times_transpose(value_grad, proj_value))
    return (
        back_inputs,
        back_rate,
        grad_in,
        grad_up,
        grad_out,
        grad_query,
        grad_key,
        grad_value,
        grad_output,
    )


def solution(mesh):
    in_specs = (
        P(("batch", "seq"), None),
        P(("batch", "seq")),
        P(),
        P(),
        P(),
        P(),
        P(),
        P(),
        P(),
        P(("batch", "seq"), None),
    )
    out_specs = (
        P(("batch", "seq"), None),
        P(("batch", "seq")),
        P("batch", None),
        P("batch", None),
        P("batch", None),
        P("seq", "batch"),
        P("seq", "batch"),
        P("seq", "batch"),
        P("batch", "seq"),
    )
    return jax.shard_map(
        functools.partial(body, mesh.shape["seq"]),
        mesh=mesh,
        in_specs=in_specs,
        out_specs=out_specs,
        check_vma=False,
    )
```

time: 501 us -> 243 us (0.49)
  waiting for transfers between devices: 331 us -> 0 us
  Pallas kernels: 0 us -> 179 us
  matrix products: 107 us -> 36.1 us
  local copies, waits for them, and re-layouts: 31.8 us -> 16.2 us
  between operations: 16 us -> 1.26 us
    psum x3 -> x0, waiting for transfers between devices: 331 us -> none  [the longest x1 163 us: body(): summed = lax.psum((contrib[0], contrib[1], contrib[2]), 'seq')]
    pallas_call x0 -> x3, Pallas kernels: none -> 179 us  [call(): pl.pallas_call(kernel, out_shape=[jax.ShapeDtypeStruct(s, d) for s, d in...]
    dot_general x45 -> x0, matrix products: 70.3 us -> none  [the longest x15 26.7 us: orthogonalize(): current = 3.4445 * current + jnp.dot(polynom, current, precision=highest)]
    unnamed x168 -> x85, local copies, waits for them, and re-layouts: 24.3 us -> 9.75 us
  transfers between devices with their start and end apart: 3 -> 0, of which waited for: 3 -> 0; matrix products, arithmetic and copies ran while one was open for 3% -> 0% of each run, Pallas kernels for 0% -> 0%
where the time goes in v1:
time: 243 us; the launch traced here: 239 us
  Pallas kernels  179 us (74%)
  matrix products  36.1 us (15%)
  local copies, waits for them, and re-layouts  16.2 us (7%)
  other arithmetic  6.02 us (2%)
    pallas_call x3, Pallas kernels, call(): pl.pallas_call(kernel, out_shape=[jax.ShapeDtypeStruct(s, d) for s, d in...  179 us
    dot_general x13, matrix products, times_transpose(): lax.dot_general(left, right, (((1,), (1,)), ((), ())), preferred_element_...  13.5 us
    dot_general x13, matrix products, token_sum(): lax.dot_general(left, right, (((0,), (0,)), ((), ())), preferred_element_...  11.6 us
    dot_general x11, matrix products, product(): return jnp.dot(left, right, preferred_element_type=jnp.float32)  11.1 us
    unnamed x85, local copies, waits for them, and re-layouts  9.75 us

profile of v1, /device:TPU:0, one launch (start us, length us, event | category | flops | bytes accessed | tf_op | source)
XLA Modules:
  0.0 238.9 jit_solution(15360890545028025687)
XLA Ops:
  0.7 1.4 copy-done
  2.1 1.6 convolution_convert_fusion.3
  3.7 0.6 convolution_convert_fusion.2
  6.4 0.8 copy-done.3
  7.6 1.0 copy-done.16
  8.6 2.7 %multiply_convert_fusion.5 = (bf16[1024,512]{1,0:T(8,128)(2,1)S(1)}, bf16[1024,512]{1,0:T(8,128)(2,1)S(1)}, bf16[1024,512]{1,0:T(8,128)(2,1)S(1)}, f32[1024,512]{1,0:T(8,128)}) fusion(f32[1024,512]{1,0:T(8,128)S(1)} %fusion.37, f32[1024,512]{1,0:T(8,128)S(1)} %fusion.34, f32[512,256]{1,0:T(8,128)S(1)} %copy-done.16, ...), kind=kOutput, calls=%fused_computation.19 | convolution fusion | flops 277217280 | bytes 10489856 | tf_op jit(solution)/shard_map/dot_general | solution.py:34
  13.0 0.9 pad_maximum_fusion
  13.9 56.4 %shard_map.169 = (bf16[256,512]{1,0:T(8,128)(2,1)}, bf16[256,512]{1,0:T(8,128)(2,1)}, bf16[512,256]{1,0:T(8,128)(2,1)}, f32[768,512]{1,0:T(8,128)}) custom-call(bf16[8,96,512]{2,1,0:T(8,128)(2,1)} %bitcast.77, f32[256,512]{1,0:T(8,128)} %fast_in.1, f32[256,512]{1,0:T(8,128)} %fast_up.1, f32[512,256]{1,0:T(8,128)} %fast_out.1), custom_call_target="tpu_custom_call" | custom-call | tf_op jit(solution)/shard_map/pallas_call | solution.py:227
  70.4 1.4 fusion.42
  72.8 2.2 multiply_convert_fusion
  75.0 1.0 copy-done.40
  76.0 1.2 convolution_convert_fusion.12
  77.2 3.9 %fusion.14 = bf16[768,256]{0,1:T(8,128)(2,1)} fusion(bf16[1024,768]{1,0:T(8,128)(2,1)} %param.19, bf16[1024,512]{1,0:T(8,128)(2,1)} %copy-done.40, bf16[512,256]{1,0:T(8,128)(2,1)} %get-tuple-element.18), kind=kOutput, calls=%fused_computation.52 | convolution fusion | flops 671547392 | bytes 3276800 | tf_op jit(solution)/shard_map/dot_general | solution.py:28
  81.1 1.6 convolution_convert_fusion.14
  84.2 0.9 pad_maximum_fusion.1
  85.8 1.2 copy.19
  87.0 64.2 %shard_map.170 = (f32[768,512]{1,0:T(8,128)}, bf16[768,512]{1,0:T(8,128)(2,1)}, f32[96,512]{1,0:T(8,128)}) custom-call(bf16[8,96,512]{2,1,0:T(8,128)(2,1)} %bitcast.76, bf16[8,96,512]{2,1,0:T(8,128)(2,1)} %bitcast.78, f32[768,512]{1,0:T(8,128)} %get-tuple-element.21.total_ref), custom_call_target="tpu_custom_call" | custom-call | tf_op jit(solution)/shard_map/pallas_call | solution.py:227
  151.2 1.9 fusion.23
  155.6 0.8 copy-done.15
  156.4 0.6 copy-done.13
  157.0 2.8 %add_convert_fusion.1 = (bf16[1024,512]{1,0:T(8,128)(2,1)S(1)}, bf16[1024,512]{1,0:T(8,128)(2,1)S(1)}, bf16[1024,512]{1,0:T(8,128)(2,1)S(1)}) fusion(f32[1024,512]{1,0:T(8,128)S(1)} %fusion.29, f32[1024,512]{1,0:T(8,128)S(1)} %copy-done.15, f32[1024,512]{1,0:T(8,128)S(1)} %copy-done.13, f32[1024,512]{1,0:T(8,128)S(1)} %fusion.18, ...), kind=kOutput, calls=%fused_computation.10 | convolution fusion | flops 285736960 | bytes 14417920 | tf_op jit(solution)/shard_map/dot_general | solution.py:24
  161.9 1.1 fusion.16
  163.5 0.9 pad_maximum_fusion.3
  165.6 1.0 pad_maximum_fusion.4
  166.5 2.3 copy.20
  168.9 58.7 %shard_map.171 = (f32[768,512]{1,0:T(8,128)}, f32[96,512]{1,0:T(8,128)}) custom-call(bf16[8,96,512]{2,1,0:T(8,128)(2,1)} %bitcast.74, bf16[8,96,512]{2,1,0:T(8,128)(2,1)} %bitcast.75), custom_call_target="tpu_custom_call" | custom-call | tf_op jit(solution)/shard_map/pallas_call | solution.py:227
  227.6 2.2 add.67
  229.8 1.2 slice_bitcast_fusion
  231.0 2.0 copy.21
  233.0 1.8 slice_bitcast_fusion.1
  234.8 1.7 fusion.46
  237.1 1.8 add_convert_fusion
  (103 shorter events, 14.0 us)
Async XLA Ops:
  0.6 1.4 copy-start
  0.7 3.0 %copy-start.18 = (bf16[768,256]{1,0:T(8,128)(2,1)S(1)}, bf16[768,256]{1,0:T(8,128)(2,1)}, u32[]{:S(2)}) copy-start(bf16[768,256]{1,0:T(8,128)(2,1)} %param.14) | copy-start | bytes 1179652
  0.7 3.6 %copy-start.32 = (bf16[768,256]{1,0:T(8,128)(2,1)S(1)}, bf16[768,256]{1,0:T(8,128)(2,1)}, u32[]{:S(2)}) copy-start(bf16[768,256]{1,0:T(8,128)(2,1)} %param.12) | copy-start | bytes 1179652
  3.6 8.6 %copy-start.7 = (bf16[1024,256]{1,0:T(8,128)(2,1)}, bf16[1024,256]{1,0:T(8,128)(2,1)S(1)}, u32[]{:S(2)}) copy-start(bf16[1024,256]{1,0:T(8,128)(2,1)S(1)} %convolution_convert_fusion.3) | copy-start | bytes 1572868
  3.7 1.6 copy-start.38
  3.7 1.6 copy-start.39
  4.3 1.6 copy-start.1
  5.3 67.0 %copy-start.27 = (bf16[1024,256]{1,0:T(8,128)(2,1)}, bf16[1024,256]{1,0:T(8,128)(2,1)S(1)}, u32[]{:S(2)}) copy-start(bf16[1024,256]{1,0:T(8,128)(2,1)S(1)} %convolution_convert_fusion.1) | copy-start | bytes 1572868
  5.9 64.5 %copy-start.29 = (bf16[1024,256]{1,0:T(8,128)(2,1)}, bf16[1024,256]{1,0:T(8,128)(2,1)S(1)}, u32[]{:S(2)}) copy-start(bf16[1024,256]{1,0:T(8,128)(2,1)S(1)} %convolution_convert_fusion.4) | copy-start | bytes 1572868
  7.2 4.1 %copy-start.12 = (f32[1024,512]{1,0:T(8,128)}, f32[1024,512]{1,0:T(8,128)S(1)}, u32[]{:S(2)}) copy-start(f32[1024,512]{1,0:T(8,128)S(1)} %fusion.34) | copy-start | bytes 6291460
  8.6 2.7 %copy-start.14 = (f32[1024,512]{1,0:T(8,128)}, f32[1024,512]{1,0:T(8,128)S(1)}, u32[]{:S(2)}) copy-start(f32[1024,512]{1,0:T(8,128)S(1)} %fusion.37) | copy-start | bytes 6291460
  11.3 1.4 copy-start.19
  11.3 1.4 copy-start.21
  11.3 1.7 copy-start.23
  70.4 1.5 copy-start.25
  72.8 3.2 %copy-start.30 = (bf16[1024,256]{1,0:T(8,128)(2,1)S(1)}, bf16[1024,256]{1,0:T(8,128)(2,1)}, u32[]{:S(2)}) copy-start(bf16[1024,256]{1,0:T(8,128)(2,1)} %copy-done.29) | copy-start | bytes 1572868
  81.1 1.6 copy-start.26
  81.1 2.1 copy-start.24
  81.1 2.1 copy-start.36
  83.7 2.0 copy-start.5
  84.2 1.6 copy-start.31
  87.0 66.1 %copy-start.22 = (bf16[1024,512]{1,0:T(8,128)(2,1)S(1)}, bf16[1024,512]{1,0:T(8,128)(2,1)}, u32[]{:S(2)}) copy-start(bf16[1024,512]{1,0:T(8,128)(2,1)} %copy-done.21) | copy-start | bytes 3145732
  151.2 1.9 copy-start.11
  151.2 2.4 copy-start.20
  153.6 1.9 copy-start.41
  154.6 1.7 copy-start.15
  155.1 1.9 copy-start.13
  157.0 2.8 %copy-start.2 = (f32[256,512]{1,0:T(8,128)S(1)}, f32[256,512]{1,0:T(8,128)}, u32[]{:S(2)}) copy-start(f32[256,512]{1,0:T(8,128)} %fast_in.1) | copy-start | bytes 1572868
  161.4 3.6 %copy-start.9 = (bf16[1024,256]{1,0:T(8,128)(2,1)}, bf16[1024,256]{1,0:T(8,128)(2,1)S(1)}, u32[]{:S(2)}) copy-start(bf16[1024,256]{1,0:T(8,128)(2,1)S(1)} %fusion.10) | copy-start | bytes 1572868
  229.8 5.0 %copy-start.10 = (bf16[1024,256]{1,0:T(8,128)(2,1)S(1)}, bf16[1024,256]{1,0:T(8,128)(2,1)}, u32[]{:S(2)}) copy-start(bf16[1024,256]{1,0:T(8,128)(2,1)} %copy-done.9) | copy-start | bytes 1572868
  234.8 1.7 copy-start.6
  234.8 1.7 copy-start.33
  (10 other events, 11.1 us)

commit v2 on v1

v2 whole, which is shorter than its diff:
```python
import functools

import jax
import jax.numpy as jnp
from jax import lax
from jax.experimental import pallas as pl
from jax.experimental.pallas import tpu as pltpu
from jax.sharding import PartitionSpec as P

NS_STEPS = 5
C1, C3, C5 = 3.4445, -4.775, 2.0315
EPS = 1e-07
MESH = pl.DeviceIdType.MESH
VMEM_LIMIT = 60 * 1024 * 1024
PAIR = 2
PASSES_FWD = 3
PASSES_BWD = 3


def rounded(value):
    return value.astype(jnp.bfloat16)


def product(left, right):
    return jnp.dot(left, right, preferred_element_type=jnp.float32)


def token_sum(left, right):
    return lax.dot_general(
        left, right, (((0,), (0,)), ((), ())), preferred_element_type=jnp.float32
    )


def times_transpose(left, right):
    return lax.dot_general(
        left, right, (((1,), (1,)), ((), ())), preferred_element_type=jnp.float32
    )


def silu_parts(pre_act):
    sigma_val = jax.nn.sigmoid(pre_act)
    activation = pre_act * sigma_val
    slope_val = sigma_val * (1.0 + pre_act * (1.0 - sigma_val))
    curvature = sigma_val * (1.0 - sigma_val) * (2.0 + pre_act * (1.0 - 2.0 * sigma_val))
    return (activation, slope_val, curvature)


def split(value, passes):
    high = rounded(value)
    if passes == 1:
        return (high,)
    return (high, rounded(value - high.astype(jnp.float32)))


def dot_split(left, right, dot):
    if len(left) == 1:
        return dot(left[0], right[0])
    along = 1 if dot is times_transpose else 0
    return dot(
        jnp.concatenate([left[0], left[0], left[1]], axis=1),
        jnp.concatenate([right[0], right[1], right[0]], axis=along),
    )


def ns_start(totals, xs):
    norms = []
    for m, matrix in enumerate(totals):
        norm = jnp.sqrt(jnp.sum(matrix * matrix))
        norms.append(norm)
        xs[0, m] = matrix / (norm + EPS)
    return norms


def ns_forward(first, last, xs, grams, polys, count, passes):
    each = range(count)

    def step(k, carry):
        xparts = [split(xs[k, m], passes) for m in each]
        gram = [dot_split(xparts[m], xparts[m], times_transpose) for m in each]
        gparts = [split(gram[m], passes) for m in each]
        poly = [C3 * gram[m] + C5 * dot_split(gparts[m], gparts[m], product) for m in each]
        pparts = [split(poly[m], passes) for m in each]
        for m in each:
            if grams is not None:
                grams[k, m] = gram[m]
                polys[k, m] = poly[m]
            xs[k + 1, m] = C1 * xs[k, m] + dot_split(pparts[m], xparts[m], product)
        return carry

    lax.fori_loop(first, last, step, 0)


def ns_backward(totals, norms, xs, grams, polys, grads, count, passes):
    each = range(count)

    def step(i, carry):
        k = NS_STEPS - 1 - i
        gparts = [split(grads[m], passes) for m in each]
        xparts = [split(xs[k, m], passes) for m in each]
        dpoly = [dot_split(gparts[m], xparts[m], times_transpose) for m in each]
        sym = [dpoly[m] + dpoly[m].T for m in each]
        twist = [
            dot_split(split(sym[m], passes), split(grams[k, m], passes), product) for m in each
        ]
        weight = [C3 * sym[m] + C5 * (twist[m] + twist[m].T) for m in each]
        for m in each:
            grads[m] = (
                C1 * grads[m]
                + dot_split(split(polys[k, m], passes), gparts[m], product)
                + dot_split(split(weight[m], passes), xparts[m], product)
            )
        return carry

    lax.fori_loop(0, NS_STEPS, step, 0)
    out = []
    for m in each:
        shifted = norms[m] + EPS
        dot_all = jnp.sum(grads[m] * totals[m])
        out.append(grads[m] / shifted - totals[m] * (dot_all / (norms[m] * shifted * shifted)))
    return out


def place():
    me = lax.axis_index("seq")
    return me // PAIR, me % PAIR


def remote(src, dst, send, recv, device):
    copy = pltpu.make_async_remote_copy(
        src_ref=src,
        dst_ref=dst,
        send_sem=send,
        recv_sem=recv,
        device_id={"seq": device},
        device_id_type=MESH,
    )
    copy.start()
    return copy


def line_peer(lines, d):
    line, side = place()
    return lax.rem(line + d, lines) * PAIR + side


def partner():
    line, side = place()
    return line * PAIR + (1 - side)


def greet(lines):
    barrier = pltpu.get_barrier_semaphore()
    for peer in [partner()] + [line_peer(lines, d) for d in range(1, lines)]:
        pl.semaphore_signal(barrier, inc=1, device_id={"seq": peer}, device_id_type=MESH)
    pl.semaphore_wait(barrier, lines)


def start_pairs(lines, src, buf):
    line, side = place()
    copies = []
    for d in list(range(1, lines)) + [0]:
        to = lax.rem(line + d, lines)
        copies.append(
            remote(
                src.at[to * PAIR + (1 - side)],
                buf.paired.at[d],
                buf.sems.at[0, d],
                buf.sems.at[1, d],
                partner(),
            )
        )
    return copies


def forward_pairs(lines, src, buf, copies):
    line, side = place()
    sent = []
    for d, copy in zip(range(1, lines), copies):
        to = lax.rem(line + d, lines)
        copy.wait()
        buf.middle[d] = rounded(
            src[to * PAIR + side].astype(jnp.float32) + buf.paired[d].astype(jnp.float32)
        )
        sent.append(
            remote(
                buf.middle.at[d],
                buf.lined.at[d],
                buf.sems.at[2, d],
                buf.sems.at[3, d],
                to * PAIR + side,
            )
        )
    return sent


def finish_scatter(lines, src, buf, copies, sent):
    copies[-1].wait()
    total = src[lax.axis_index("seq")].astype(jnp.float32) + buf.paired[0].astype(jnp.float32)
    for d, copy in zip(range(1, lines), sent):
        copy.wait()
        total = total + buf.lined[d].astype(jnp.float32)
    return total


def start_gather(lines, buf):
    out = []
    for d in range(1, lines):
        out.append(
            remote(
                buf.mine,
                buf.gathered.at[d],
                buf.sems.at[4, d],
                buf.sems.at[5, d],
                line_peer(lines, d),
            )
        )
    across = remote(buf.mine, buf.crossed.at[0], buf.sems.at[6, 0], buf.sems.at[7, 0], partner())
    return out, [across]


def finish_gather(lines, buf, copies, full):
    line, side = place()
    rows = buf.mine.shape[0]
    out, across = copies

    def put(owner, block):
        full[pl.ds(pl.multiple_of(owner * rows, rows), rows), :] = block.astype(jnp.float32)

    for d in range(1, lines):
        out[d - 1].wait()
        across.append(
            remote(
                buf.gathered.at[d],
                buf.crossed.at[d],
                buf.sems.at[6, d],
                buf.sems.at[7, d],
                partner(),
            )
        )
    put(line * PAIR + side, buf.mine[...])
    for d in range(1, lines):
        put(lax.rem(line - d + lines, lines) * PAIR + side, buf.gathered[d])
    for d in range(lines):
        across[d].wait()
        put(lax.rem(line - d + lines, lines) * PAIR + (1 - side), buf.crossed[d])


class Scatter:
    def __init__(self, paired, middle, lined, sems):
        self.paired, self.middle, self.lined, self.sems = paired, middle, lined, sems

    @staticmethod
    def scratch(lines, block):
        slots = pltpu.VMEM((lines,) + block, jnp.bfloat16)
        return [slots, slots, slots, pltpu.SemaphoreType.DMA((4, lines))]


class Reduce(Scatter):
    def __init__(self, paired, middle, lined, mine, gathered, crossed, sems):
        super().__init__(paired, middle, lined, sems)
        self.mine, self.gathered, self.crossed = mine, gathered, crossed

    @staticmethod
    def scratch(lines, block):
        slots = pltpu.VMEM((lines,) + block, jnp.bfloat16)
        one = pltpu.VMEM(block, jnp.bfloat16)
        return [slots, slots, slots, one, slots, slots, pltpu.SemaphoreType.DMA((8, lines))]


def forward_kernel(
    lines, count, part, fast_in, fast_up, fast_out, n_in, n_up, n_out, total_out, *scratch
):
    buf, xs = Reduce(*scratch[:7]), scratch[7]
    greet(lines)
    copies = start_pairs(lines, part, buf)
    sent = forward_pairs(lines, part, buf, copies)
    buf.mine[...] = rounded(finish_scatter(lines, part, buf, copies, sent))
    finish_gather(lines, buf, start_gather(lines, buf), total_out)
    h = total_out.shape[0] // count
    totals = [total_out[m * h : (m + 1) * h, :] for m in range(count)]
    ns_start(totals, xs)
    ns_forward(0, NS_STEPS, xs, None, None, count, PASSES_FWD)
    n_in[...] = rounded(fast_in[...] + xs[NS_STEPS, 0])
    n_up[...] = rounded(fast_up[...] + xs[NS_STEPS, 1])
    n_out[...] = rounded(fast_out[...] + xs[NS_STEPS, 2].T)


def backward_kernel(
    lines, count, part, rows_part, total_ref, adjoint_out, back_out, rows_out, *scratch
):
    buf, row_buf = Reduce(*scratch[:7]), Scatter(*scratch[7:11])
    xs, grams, polys, grads = scratch[11:]
    greet(lines)
    copies = start_pairs(lines, part, buf)
    h = total_ref.shape[0] // count
    totals = [total_ref[m * h : (m + 1) * h, :] for m in range(count)]
    norms = ns_start(totals, xs)
    ns_forward(0, NS_STEPS - 4, xs, grams, polys, count, PASSES_FWD)
    sent = forward_pairs(lines, part, buf, copies)
    ns_forward(NS_STEPS - 4, NS_STEPS - 2, xs, grams, polys, count, PASSES_FWD)
    buf.mine[...] = rounded(finish_scatter(lines, part, buf, copies, sent))
    gathering = start_gather(lines, buf)
    ns_forward(NS_STEPS - 2, NS_STEPS, xs, grams, polys, count, PASSES_FWD)
    finish_gather(lines, buf, gathering, adjoint_out)
    copies = start_pairs(lines, rows_part, row_buf)
    sent = forward_pairs(lines, rows_part, row_buf, copies)
    for m in range(count):
        grads[m] = adjoint_out[m * h : (m + 1) * h, :]
    result = ns_backward(totals, norms, xs, grams, polys, grads, count, PASSES_BWD)
    for m in range(count):
        back_out[m * h : (m + 1) * h, :] = rounded(result[m])
    rows_out[...] = finish_scatter(lines, rows_part, row_buf, copies, sent)


def final_kernel(lines, part, rows_part, sum_out, rows_out, *scratch):
    buf, row_buf = Reduce(*scratch[:7]), Scatter(*scratch[7:11])
    greet(lines)
    copies = start_pairs(lines, part, buf)
    row_copies = start_pairs(lines, rows_part, row_buf)
    sent = forward_pairs(lines, part, buf, copies)
    buf.mine[...] = rounded(finish_scatter(lines, part, buf, copies, sent))
    row_sent = forward_pairs(lines, rows_part, row_buf, row_copies)
    gathering = start_gather(lines, buf)
    rows_out[...] = finish_scatter(lines, rows_part, row_buf, row_copies, row_sent)
    finish_gather(lines, buf, gathering, sum_out)


def call(kernel, identity, outs, scratch, *operands):
    vmem = pl.BlockSpec(memory_space=pltpu.VMEM)
    return pl.pallas_call(
        kernel,
        out_shape=[jax.ShapeDtypeStruct(s, d) for s, d in outs],
        in_specs=[vmem] * len(operands),
        out_specs=[vmem] * len(outs),
        scratch_shapes=scratch,
        compiler_params=pltpu.CompilerParams(
            collective_id=identity, has_side_effects=True, vmem_limit_bytes=VMEM_LIMIT
        ),
    )(*operands)


def body(
    n,
    inputs,
    token_rates,
    proj_query,
    proj_key,
    proj_value,
    proj_output,
    fast_in,
    fast_up,
    fast_out,
    cotangent,
):
    bf16, f32 = jnp.bfloat16, jnp.float32
    h, f = fast_in.shape
    width = inputs.shape[1]
    count = 3
    block = (count * h // n, f)
    row_block = (width // n, 2 * h)

    query_rows = rounded(product(inputs, proj_query))
    key_rows = rounded(product(inputs, proj_key))
    value_rows = rounded(product(inputs, proj_value))
    w_in, w_up, w_out = (rounded(fast_in), rounded(fast_up), rounded(fast_out))
    scaled = rounded(token_rates[:, None] * value_rows.astype(f32))
    pre_in = product(key_rows, w_in)
    pre_up = product(key_rows, w_up)
    activation, slope_val, curvature = silu_parts(pre_in)
    hidden = rounded(activation * pre_up)
    upstream = times_transpose(scaled, w_out)
    grad_in_rows = rounded(upstream * pre_up * slope_val)
    grad_up_rows = rounded(upstream * activation)

    def stacked(*terms):
        return jnp.concatenate([rounded(t) for t in terms]).reshape((n,) + block)

    def row_stacked(left, right):
        return jnp.concatenate([rounded(left), rounded(right)], axis=1).reshape((n,) + row_block)

    part = stacked(
        token_sum(key_rows, grad_in_rows),
        token_sum(key_rows, grad_up_rows),
        token_sum(scaled, hidden),
    )
    lines = n // PAIR
    exchange = Reduce.scratch(lines, block)
    row_scratch = Scatter.scratch(lines, row_block)
    n_in, n_up, n_out, totals = call(
        functools.partial(forward_kernel, lines, count),
        0,
        [((h, f), bf16), ((h, f), bf16), ((f, h), bf16), ((count * h, f), f32)],
        exchange + [pltpu.VMEM((NS_STEPS + 1, count, h, f), f32)],
        part, fast_in, fast_up, fast_out,
    )

    pre_p = product(query_rows, n_in)
    pre_r = product(query_rows, n_up)
    activation_q, slope_q, _ = silu_parts(pre_p)
    hidden_q = rounded(activation_q * pre_r)
    output_rows = rounded(product(hidden_q, n_out))
    back_output = rounded(times_transpose(cotangent, proj_output))
    back_hidden = times_transpose(back_output, n_out)
    back_p = rounded(back_hidden * pre_r * slope_q)
    back_r = rounded(back_hidden * activation_q)
    query_grad = rounded(times_transpose(back_p, n_in) + times_transpose(back_r, n_up))
    part = stacked(
        token_sum(query_rows, back_p),
        token_sum(query_rows, back_r),
        token_sum(back_output, hidden_q),
    )
    rows_part = row_stacked(token_sum(inputs, query_grad), token_sum(cotangent, output_rows))
    adjoint, back_totals, rows_sum = call(
        functools.partial(backward_kernel, lines, count),
        1,
        [((count * h, f), f32), ((count * h, f), bf16), (row_block, f32)],
        exchange
        + row_scratch
        + [
            pltpu.VMEM((NS_STEPS + 1, count, h, f), f32),
            pltpu.VMEM((NS_STEPS, count, h, h), f32),
            pltpu.VMEM((NS_STEPS, count, h, h), f32),
            pltpu.VMEM((count, h, f), f32),
        ],
        part, rows_part, totals,
    )
    grad_query = rows_sum[:, :h]
    grad_output = rows_sum[:, h:].T

    b_in, b_up, b_out = (back_totals[m * h : (m + 1) * h] for m in range(count))
    press_in = product(key_rows, b_in)
    press_up = product(key_rows, b_up)
    back_hid = product(scaled, b_out)
    back_upstream = rounded(press_in * pre_up * slope_val + press_up * activation)
    back_pre_up = rounded(press_in * upstream * slope_val + back_hid * activation)
    back_pre_in = rounded(
        press_in * upstream * pre_up * curvature
        + press_up * upstream * slope_val
        + back_hid * pre_up * slope_val
    )
    back_scaled = times_transpose(hidden, b_out) + product(back_upstream, w_out)
    back_rate = jnp.sum(back_scaled * value_rows.astype(f32), axis=1)
    key_sum = times_transpose(grad_in_rows, b_in) + times_transpose(grad_up_rows, b_up)
    key_sum = key_sum + times_transpose(back_pre_in, w_in) + times_transpose(back_pre_up, w_up)
    key_grad = rounded(key_sum)
    value_grad = rounded(token_rates[:, None] * back_scaled)
    part = stacked(
        token_sum(key_rows, back_pre_in),
        token_sum(key_rows, back_pre_up),
        token_sum(scaled, back_upstream),
    )
    rows_part = row_stacked(token_sum(inputs, key_grad), token_sum(inputs, value_grad))
    summed, rows_sum = call(
        functools.partial(final_kernel, lines),
        2,
        [((count * h, f), f32), (row_block, f32)],
        exchange + row_scratch,
        part, rows_part,
    )
    grad_key = rows_sum[:, :h]
    grad_value = rows_sum[:, h:]
    both = adjoint + summed
    grad_in = both[:h]
    grad_up = both[h : 2 * h]
    grad_out = both[2 * h :].T
    total = times_transpose(query_grad, proj_query) + times_transpose(key_grad, proj_key)
    back_inputs = rounded(total + times_transpose(value_grad, proj_value))
    return (
        back_inputs,
        back_rate,
        grad_in,
        grad_up,
        grad_out,
        grad_query,
        grad_key,
        grad_value,
        grad_output,
    )


def solution(mesh):
    in_specs = (
        P(("batch", "seq"), None),
        P(("batch", "seq")),
        P(),
        P(),
        P(),
        P(),
        P(),
        P(),
        P(),
        P(("batch", "seq"), None),
    )
    out_specs = (
        P(("batch", "seq"), None),
        P(("batch", "seq")),
        P("batch", None),
        P("batch", None),
        P("batch", None),
        P("seq", "batch"),
        P("seq", "batch"),
        P("seq", "batch"),
        P("batch", "seq"),
    )
    return jax.shard_map(
        functools.partial(body, mesh.shape["seq"]),
        mesh=mesh,
        in_specs=in_specs,
        out_specs=out_specs,
        check_vma=False,
    )
```

time: 243 us -> 198 us (0.81); the launches traced: 239 us -> 197 us
  Pallas kernels: 179 us -> 138 us
    pallas_call x3, Pallas kernels: 179 us -> 138 us  [call(): pl.pallas_call(kernel, out_shape=[jax.ShapeDtypeStruct(s, d) for s, d in...]
where the time goes in v2:
time: 198 us; the launch traced here: 197 us
  Pallas kernels  138 us (70%)
  matrix products  36.1 us (18%)
  local copies, waits for them, and re-layouts  16.2 us (8%)
  other arithmetic  6.02 us (3%)
    pallas_call x3, Pallas kernels, call(): pl.pallas_call(kernel, out_shape=[jax.ShapeDtypeStruct(s, d) for s, d in...  138 us
    dot_general x13, matrix products, times_transpose(): lax.dot_general(left, right, (((1,), (1,)), ((), ())), preferred_element_...  13.5 us
    dot_general x13, matrix products, token_sum(): lax.dot_general(left, right, (((0,), (0,)), ((), ())), preferred_element_...  11.6 us
    dot_general x11, matrix products, product(): return jnp.dot(left, right, preferred_element_type=jnp.float32)  11.1 us
    unnamed x85, local copies, waits for them, and re-layouts  9.76 us

profile of v2, /device:TPU:0, one launch (start us, length us, event | category | flops | bytes accessed | tf_op | source)
XLA Modules:
  0.0 197.2 jit_solution(17399504283689969649)
XLA Ops:
  0.7 1.4 copy-done
  2.1 1.6 convolution_convert_fusion.3
  3.7 0.6 convolution_convert_fusion.2
  6.4 0.8 copy-done.3
  7.6 1.0 copy-done.16
  8.6 2.7 %multiply_convert_fusion.5 = (bf16[1024,512]{1,0:T(8,128)(2,1)S(1)}, bf16[1024,512]{1,0:T(8,128)(2,1)S(1)}, bf16[1024,512]{1,0:T(8,128)(2,1)S(1)}, f32[1024,512]{1,0:T(8,128)}) fusion(f32[1024,512]{1,0:T(8,128)S(1)} %fusion.37, f32[1024,512]{1,0:T(8,128)S(1)} %fusion.34, f32[512,256]{1,0:T(8,128)S(1)} %copy-done.16, ...), kind=kOutput, calls=%fused_computation.19 | convolution fusion | flops 277217280 | bytes 10489856 | tf_op jit(solution)/shard_map/dot_general | solution.py:35
  13.0 0.9 pad_maximum_fusion
  13.9 43.1 %shard_map.169 = (bf16[256,512]{1,0:T(8,128)(2,1)}, bf16[256,512]{1,0:T(8,128)(2,1)}, bf16[512,256]{1,0:T(8,128)(2,1)}, f32[768,512]{1,0:T(8,128)}) custom-call(bf16[8,96,512]{2,1,0:T(8,128)(2,1)} %bitcast.77, f32[256,512]{1,0:T(8,128)} %fast_in.1, f32[256,512]{1,0:T(8,128)} %fast_up.1, f32[512,256]{1,0:T(8,128)} %fast_out.1), custom_call_target="tpu_custom_call" | custom-call | tf_op jit(solution)/shard_map/pallas_call | solution.py:330
  57.1 1.4 fusion.42
  59.5 2.2 %multiply_convert_fusion = (bf16[1024,512]{1,0:T(8,128)(2,1)S(1)}, bf16[1024,512]{1,0:T(8,128)(2,1)S(1)}, bf16[1024,512]{1,0:T(8,128)(2,1)}) fusion(f32[1024,512]{1,0:T(8,128)S(1)} %fusion.43, f32[1024,512]{1,0:T(8,128)S(1)} %fusion.42, bf16[1024,256]{1,0:T(8,128)(2,1)S(1)} %convolution_convert_fusion.1, bf16[256,512]{1,0:T(8,128)(2,1)S(1)} %copy-done.35), kind=kOutput, calls=%fused_computation.12 | convolution fusion | flops 276299776 | bytes 8126464 | tf_op jit(solution)/shard_map/dot_general | solution.py:25
  61.7 1.0 copy-done.40
  62.7 1.2 convolution_convert_fusion.12
  63.8 3.9 %fusion.14 = bf16[768,256]{0,1:T(8,128)(2,1)} fusion(bf16[1024,768]{1,0:T(8,128)(2,1)} %param.19, bf16[1024,512]{1,0:T(8,128)(2,1)} %copy-done.40, bf16[512,256]{1,0:T(8,128)(2,1)} %get-tuple-element.18), kind=kOutput, calls=%fused_computation.52 | convolution fusion | flops 671547392 | bytes 3276800 | tf_op jit(solution)/shard_map/dot_general | solution.py:29
  67.7 1.6 convolution_convert_fusion.14
  70.9 0.9 pad_maximum_fusion.1
  72.5 1.2 copy.19
  73.7 57.7 %shard_map.170 = (f32[768,512]{1,0:T(8,128)}, bf16[768,512]{1,0:T(8,128)(2,1)}, f32[96,512]{1,0:T(8,128)}) custom-call(bf16[8,96,512]{2,1,0:T(8,128)(2,1)} %bitcast.76, bf16[8,96,512]{2,1,0:T(8,128)(2,1)} %bitcast.78, f32[768,512]{1,0:T(8,128)} %get-tuple-element.21.total_ref), custom_call_target="tpu_custom_call" | custom-call | tf_op jit(solution)/shard_map/pallas_call | solution.py:330
  131.4 1.9 fusion.23
  135.7 0.8 copy-done.15
  136.5 0.6 copy-done.13
  137.1 2.8 %add_convert_fusion.1 = (bf16[1024,512]{1,0:T(8,128)(2,1)S(1)}, bf16[1024,512]{1,0:T(8,128)(2,1)S(1)}, bf16[1024,512]{1,0:T(8,128)(2,1)S(1)}) fusion(f32[1024,512]{1,0:T(8,128)S(1)} %fusion.29, f32[1024,512]{1,0:T(8,128)S(1)} %copy-done.15, f32[1024,512]{1,0:T(8,128)S(1)} %copy-done.13, f32[1024,512]{1,0:T(8,128)S(1)} %fusion.18, ...), kind=kOutput, calls=%fused_computation.10 | convolution fusion | flops 285736960 | bytes 14417920 | tf_op jit(solution)/shard_map/dot_general | solution.py:25
  142.1 1.1 fusion.16
  143.6 0.9 pad_maximum_fusion.3
  145.7 1.0 pad_maximum_fusion.4
  146.7 2.3 %copy.20 = bf16[768,512]{1,0:T(8,128)(2,1)} copy(bf16[768,512]{0,1:T(8,128)(2,1)} %pad_maximum_fusion.4) | data formatting | bytes 1572864 | tf_op jit(solution)/shard_map/concatenate | solution.py:379
  149.0 36.8 %shard_map.171 = (f32[768,512]{1,0:T(8,128)}, f32[96,512]{1,0:T(8,128)}) custom-call(bf16[8,96,512]{2,1,0:T(8,128)(2,1)} %bitcast.74, bf16[8,96,512]{2,1,0:T(8,128)(2,1)} %bitcast.75), custom_call_target="tpu_custom_call" | custom-call | tf_op jit(solution)/shard_map/pallas_call | solution.py:330
  185.8 2.2 %add.67 = f32[768,512]{1,0:T(8,128)S(1)} add(f32[768,512]{1,0:T(8,128)} %get-tuple-element.23, f32[768,512]{1,0:T(8,128)} %get-tuple-element.24) | non-fusion elementwise | flops 393216 | bytes 4718592 | tf_op jit(solution)/shard_map/add | solution.py:462
  188.1 1.2 slice_bitcast_fusion
  189.2 2.0 %copy.21 = f32[512,256]{1,0:T(8,128)} copy(f32[512,256]{0,1:T(8,128)} %get-tuple-element.45) | data formatting | bytes 1048576
  191.3 1.8 slice_bitcast_fusion.1
  193.1 1.7 fusion.46
  195.4 1.8 add_convert_fusion
  (103 shorter events, 13.9 us)
Async XLA Ops:
  0.6 1.4 copy-start
  0.7 3.0 %copy-start.18 = (bf16[768,256]{1,0:T(8,128)(2,1)S(1)}, bf16[768,256]{1,0:T(8,128)(2,1)}, u32[]{:S(2)}) copy-start(bf16[768,256]{1,0:T(8,128)(2,1)} %param.14) | copy-start | bytes 1179652
  0.7 3.6 %copy-start.32 = (bf16[768,256]{1,0:T(8,128)(2,1)S(1)}, bf16[768,256]{1,0:T(8,128)(2,1)}, u32[]{:S(2)}) copy-start(bf16[768,256]{1,0:T(8,128)(2,1)} %param.12) | copy-start | bytes 1179652
  3.6 8.6 %copy-start.7 = (bf16[1024,256]{1,0:T(8,128)(2,1)}, bf16[1024,256]{1,0:T(8,128)(2,1)S(1)}, u32[]{:S(2)}) copy-start(bf16[1024,256]{1,0:T(8,128)(2,1)S(1)} %convolution_convert_fusion.3) | copy-start | bytes 1572868
  3.7 1.6 copy-start.38
  3.7 1.6 copy-start.39
  4.3 1.6 copy-start.1
  5.3 53.7 %copy-start.27 = (bf16[1024,256]{1,0:T(8,128)(2,1)}, bf16[1024,256]{1,0:T(8,128)(2,1)S(1)}, u32[]{:S(2)}) copy-start(bf16[1024,256]{1,0:T(8,128)(2,1)S(1)} %convolution_convert_fusion.1) | copy-start | bytes 1572868
  5.9 51.1 %copy-start.29 = (bf16[1024,256]{1,0:T(8,128)(2,1)}, bf16[1024,256]{1,0:T(8,128)(2,1)S(1)}, u32[]{:S(2)}) copy-start(bf16[1024,256]{1,0:T(8,128)(2,1)S(1)} %convolution_convert_fusion.4) | copy-start | bytes 1572868
  7.2 4.1 %copy-start.12 = (f32[1024,512]{1,0:T(8,128)}, f32[1024,512]{1,0:T(8,128)S(1)}, u32[]{:S(2)}) copy-start(f32[1024,512]{1,0:T(8,128)S(1)} %fusion.34) | copy-start | bytes 6291460
  8.6 2.7 %copy-start.14 = (f32[1024,512]{1,0:T(8,128)}, f32[1024,512]{1,0:T(8,128)S(1)}, u32[]{:S(2)}) copy-start(f32[1024,512]{1,0:T(8,128)S(1)} %fusion.37) | copy-start | bytes 6291460
  11.3 1.4 copy-start.19
  11.3 1.4 copy-start.21
  11.3 1.7 copy-start.23
  57.1 1.5 copy-start.25
  59.5 3.2 %copy-start.30 = (bf16[1024,256]{1,0:T(8,128)(2,1)S(1)}, bf16[1024,256]{1,0:T(8,128)(2,1)}, u32[]{:S(2)}) copy-start(bf16[1024,256]{1,0:T(8,128)(2,1)} %copy-done.29) | copy-start | bytes 1572868
  67.7 1.6 copy-start.26
  67.7 2.1 %copy-start.24 = (bf16[1024,512]{1,0:T(8,128)(2,1)S(1)}, bf16[1024,512]{1,0:T(8,128)(2,1)}, u32[]{:S(2)}) copy-start(bf16[1024,512]{1,0:T(8,128)(2,1)} %get-tuple-element.41) | copy-start | bytes 3145732
  67.7 2.1 %copy-start.36 = (bf16[256,512]{1,0:T(8,128)(2,1)S(1)}, bf16[256,512]{1,0:T(8,128)(2,1)}, u32[]{:S(2)}) copy-start(bf16[256,512]{1,0:T(8,128)(2,1)} %get-tuple-element.19) | copy-start | bytes 786436
  70.4 2.0 %copy-start.5 = (bf16[1024,256]{1,0:T(8,128)(2,1)}, bf16[1024,256]{1,0:T(8,128)(2,1)S(1)}, u32[]{:S(2)}) copy-start(bf16[1024,256]{1,0:T(8,128)(2,1)S(1)} %fusion.9) | copy-start | bytes 1572868
  70.9 1.6 copy-start.31
  73.7 59.6 %copy-start.22 = (bf16[1024,512]{1,0:T(8,128)(2,1)S(1)}, bf16[1024,512]{1,0:T(8,128)(2,1)}, u32[]{:S(2)}) copy-start(bf16[1024,512]{1,0:T(8,128)(2,1)} %copy-done.21) | copy-start | bytes 3145732
  131.3 1.9 copy-start.11
  131.3 2.4 %copy-start.20 = (bf16[1024,512]{1,0:T(8,128)(2,1)S(1)}, bf16[1024,512]{1,0:T(8,128)(2,1)}, u32[]{:S(2)}) copy-start(bf16[1024,512]{1,0:T(8,128)(2,1)} %copy-done.19) | copy-start | bytes 3145732
  133.7 1.9 copy-start.41
  134.8 1.7 copy-start.15
  135.2 1.9 copy-start.13
  137.1 2.8 %copy-start.2 = (f32[256,512]{1,0:T(8,128)S(1)}, f32[256,512]{1,0:T(8,128)}, u32[]{:S(2)}) copy-start(f32[256,512]{1,0:T(8,128)} %fast_in.1) | copy-start | bytes 1572868
  141.5 3.6 %copy-start.9 = (bf16[1024,256]{1,0:T(8,128)(2,1)}, bf16[1024,256]{1,0:T(8,128)(2,1)S(1)}, u32[]{:S(2)}) copy-start(bf16[1024,256]{1,0:T(8,128)(2,1)S(1)} %fusion.10) | copy-start | bytes 1572868
  188.1 5.0 %copy-start.10 = (bf16[1024,256]{1,0:T(8,128)(2,1)S(1)}, bf16[1024,256]{1,0:T(8,128)(2,1)}, u32[]{:S(2)}) copy-start(bf16[1024,256]{1,0:T(8,128)(2,1)} %copy-done.9) | copy-start | bytes 1572868
  193.1 1.7 copy-start.6
  193.1 1.7 copy-start.33
  (10 other events, 11.1 us)

commit v3 on v2

--- a/solution.py
+++ b/solution.py
@@ -1,4 +1,5 @@
 import functools
+import math
 
 import jax
 import jax.numpy as jnp
@@ -90,7 +91,7 @@
     lax.fori_loop(first, last, step, 0)
 
 
-def ns_backward(totals, norms, xs, grams, polys, grads, count, passes):
+def ns_backward(first, last, xs, grams, polys, grads, count, passes):
     each = range(count)
 
     def step(i, carry):
@@ -111,9 +112,12 @@
             )
         return carry
 
-    lax.fori_loop(0, NS_STEPS, step, 0)
+    lax.fori_loop(first, last, step, 0)
+
+
+def ns_finish(totals, norms, grads, count):
     out = []
-    for m in each:
+    for m in range(count):
         shifted = norms[m] + EPS
         dot_all = jnp.sum(grads[m] * totals[m])
         out.append(grads[m] / shifted - totals[m] * (dot_all / (norms[m] * shifted * shifted)))
@@ -218,14 +222,8 @@
     return out, [across]
 
 
-def finish_gather(lines, buf, copies, full):
-    line, side = place()
-    rows = buf.mine.shape[0]
+def relay_gather(lines, buf, copies):
     out, across = copies
-
-    def put(owner, block):
-        full[pl.ds(pl.multiple_of(owner * rows, rows), rows), :] = block.astype(jnp.float32)
-
     for d in range(1, lines):
         out[d - 1].wait()
         across.append(
@@ -237,6 +235,16 @@
                 partner(),
             )
         )
+
+
+def finish_gather(lines, buf, copies, full):
+    line, side = place()
+    rows = buf.mine.shape[0]
+    across = copies[1]
+
+    def put(owner, block):
+        full[pl.ds(pl.multiple_of(owner * rows, rows), rows), :] = block.astype(jnp.float32)
+
     put(line * PAIR + side, buf.mine[...])
     for d in range(1, lines):
         put(lax.rem(line - d + lines, lines) * PAIR + side, buf.gathered[d])
@@ -275,7 +283,9 @@
     copies = start_pairs(lines, part, buf)
     sent = forward_pairs(lines, part, buf, copies)
     buf.mine[...] = rounded(finish_scatter(lines, part, buf, copies, sent))
-    finish_gather(lines, buf, start_gather(lines, buf), total_out)
+    gathering = start_gather(lines, buf)
+    relay_gather(lines, buf, gathering)
+    finish_gather(lines, buf, gathering, total_out)
     h = total_out.shape[0] // count
     totals = [total_out[m * h : (m + 1) * h, :] for m in range(count)]
     ns_start(totals, xs)
@@ -285,44 +295,84 @@
     n_out[...] = rounded(fast_out[...] + xs[NS_STEPS, 2].T)
 
 
+def fill_rows(rows_part, pairs):
+    n, rows = rows_part.shape[:2]
+    at = 0
+    for left, right in pairs:
+        total = token_sum(left[...], right[...])
+        wide = total.shape[1]
+        for j in range(n):
+            rows_part[j, :, at : at + wide] = rounded(total[j * rows : (j + 1) * rows, :])
+        at += wide
+
+
 def backward_kernel(
-    lines, count, part, rows_part, total_ref, adjoint_out, back_out, rows_out, *scratch
+    lines, count, part, inputs, query_grad, cotangent, output_rows, total_ref,
+    adjoint_out, back_out, rows_out, *scratch
 ):
     buf, row_buf = Reduce(*scratch[:7]), Scatter(*scratch[7:11])
-    xs, grams, polys, grads = scratch[11:]
+    rows_part, xs, grams, polys, grads = scratch[11:]
     greet(lines)
     copies = start_pairs(lines, part, buf)
     h = total_ref.shape[0] // count
     totals = [total_ref[m * h : (m + 1) * h, :] for m in range(count)]
     norms = ns_start(totals, xs)
+    fill_rows(rows_part, ((inputs, query_grad), (cotangent, output_rows)))
     ns_forward(0, NS_STEPS - 4, xs, grams, polys, count, PASSES_FWD)
     sent = forward_pairs(lines, part, buf, copies)
     ns_forward(NS_STEPS - 4, NS_STEPS - 2, xs, grams, polys, count, PASSES_FWD)
     buf.mine[...] = rounded(finish_scatter(lines, part, buf, copies, sent))
     gathering = start_gather(lines, buf)
     ns_forward(NS_STEPS - 2, NS_STEPS, xs, grams, polys, count, PASSES_FWD)
+    relay_gather(lines, buf, gathering)
     finish_gather(lines, buf, gathering, adjoint_out)
     copies = start_pairs(lines, rows_part, row_buf)
-    sent = forward_pairs(lines, rows_part, row_buf, copies)
     for m in range(count):
         grads[m] = adjoint_out[m * h : (m + 1) * h, :]
-    result = ns_backward(totals, norms, xs, grams, polys, grads, count, PASSES_BWD)
+    ns_backward(0, NS_STEPS - 2, xs, grams, polys, grads, count, PASSES_BWD)
+    sent = forward_pairs(lines, rows_part, row_buf, copies)
+    ns_backward(NS_STEPS - 2, NS_STEPS, xs, grams, polys, grads, count, PASSES_BWD)
+    result = ns_finish(totals, norms, grads, count)
     for m in range(count):
         back_out[m * h : (m + 1) * h, :] = rounded(result[m])
     rows_out[...] = finish_scatter(lines, rows_part, row_buf, copies, sent)
 
 
-def final_kernel(lines, part, rows_part, sum_out, rows_out, *scratch):
+def final_kernel(
+    lines, count, part, inputs, query_grad, key_grad, value_grad,
+    proj_query, proj_key, proj_value, adjoint,
+    grad_in, grad_up, grad_out, grad_key, grad_value, back_inputs, *scratch
+):
     buf, row_buf = Reduce(*scratch[:7]), Scatter(*scratch[7:11])
+    rows_part, total = scratch[11:]
     greet(lines)
     copies = start_pairs(lines, part, buf)
+    fill_rows(rows_part, ((inputs, key_grad), (inputs, value_grad)))
     row_copies = start_pairs(lines, rows_part, row_buf)
     sent = forward_pairs(lines, part, buf, copies)
     buf.mine[...] = rounded(finish_scatter(lines, part, buf, copies, sent))
+    gathering = start_gather(lines, buf)
     row_sent = forward_pairs(lines, rows_part, row_buf, row_copies)
-    gathering = start_gather(lines, buf)
-    rows_out[...] = finish_scatter(lines, rows_part, row_buf, row_copies, row_sent)
-    finish_gather(lines, buf, gathering, sum_out)
+    relay_gather(lines, buf, gathering)
+
+    tile = math.gcd(inputs.shape[0], 256)
+    weights = jnp.concatenate([proj_query[...], proj_key[...], proj_value[...]], axis=1)
+
+    def tokens(i, carry):
+        at = pl.ds(pl.multiple_of(i * tile, tile), tile)
+        grads = jnp.concatenate([query_grad[at, :], key_grad[at, :], value_grad[at, :]], axis=1)
+        back_inputs[at, :] = rounded(times_transpose(grads, weights))
+        return carry
+
+    lax.fori_loop(0, inputs.shape[0] // tile, tokens, 0)
+    sums = finish_scatter(lines, rows_part, row_buf, row_copies, row_sent)
+    h = key_grad.shape[1]
+    grad_key[...] = sums[:, :h]
+    grad_value[...] = sums[:, h:]
+    finish_gather(lines, buf, gathering, total)
+    grad_in[...] = adjoint[:h, :] + total[:h, :]
+    grad_up[...] = adjoint[h : 2 * h, :] + total[h : 2 * h, :]
+    grad_out[...] = (adjoint[2 * h :, :] + total[2 * h :, :]).T
 
 
 def call(kernel, identity, outs, scratch, *operands):
@@ -375,9 +425,6 @@
     def stacked(*terms):
         return jnp.concatenate([rounded(t) for t in terms]).reshape((n,) + block)
 
-    def row_stacked(left, right):
-        return jnp.concatenate([rounded(left), rounded(right)], axis=1).reshape((n,) + row_block)
-
     part = stacked(
         token_sum(key_rows, grad_in_rows),
         token_sum(key_rows, grad_up_rows),
@@ -409,7 +456,6 @@
         token_sum(query_rows, back_r),
         token_sum(back_output, hidden_q),
     )
-    rows_part = row_stacked(token_sum(inputs, query_grad), token_sum(cotangent, output_rows))
     adjoint, back_totals, rows_sum = call(
         functools.partial(backward_kernel, lines, count),
         1,
@@ -417,12 +463,13 @@
         exchange
         + row_scratch
         + [
+            pltpu.VMEM((n,) + row_block, bf16),
             pltpu.VMEM((NS_STEPS + 1, count, h, f), f32),
             pltpu.VMEM((NS_STEPS, count, h, h), f32),
             pltpu.VMEM((NS_STEPS, count, h, h), f32),
             pltpu.VMEM((count, h, f), f32),
         ],
-        part, rows_part, totals,
+        part, inputs, query_grad, cotangent, output_rows, totals,
     )
     grad_query = rows_sum[:, :h]
     grad_output = rows_sum[:, h:].T
@@ -449,22 +496,23 @@
         token_sum(key_rows, back_pre_up),
         token_sum(scaled, back_upstream),
     )
-    rows_part = row_stacked(token_sum(inputs, key_grad), token_sum(inputs, value_grad))
-    summed, rows_sum = call(
-        functools.partial(final_kernel, lines),
+    grad_in, grad_up, grad_out, grad_key, grad_value, back_inputs = call(
+        functools.partial(final_kernel, lines, count),
         2,
-        [((count * h, f), f32), (row_block, f32)],
-        exchange + row_scratch,
-        part, rows_part,
-    )
-    grad_key = rows_sum[:, :h]
-    grad_value = rows_sum[:, h:]
-    both = adjoint + summed
-    grad_in = both[:h]
-    grad_up = both[h : 2 * h]
-    grad_out = both[2 * h :].T
-    total = times_transpose(query_grad, proj_query) + times_transpose(key_grad, proj_key)
-    back_inputs = rounded(total + times_transpose(value_grad, proj_value))
+        [
+            ((h, f), f32),
+            ((h, f), f32),
+            ((f, h), f32),
+            ((width // n, h), f32),
+            ((width // n, h), f32),
+            (inputs.shape, bf16),
+        ],
+        exchange
+        + row_scratch
+        + [pltpu.VMEM((n,) + row_block, bf16), pltpu.VMEM((count * h, f), f32)],
+        part, inputs, query_grad, key_grad, value_grad,
+        proj_query, proj_key, proj_value, adjoint,
+    )
     return (
         back_inputs,
         back_rate,

time: 198 us -> 178 us (0.90)
  Pallas kernels: 138 us -> 131 us
  matrix products: 36.1 us -> 30.1 us
  local copies, waits for them, and re-layouts: 16.2 us -> 11.7 us
  other arithmetic: 6.02 us -> 2.88 us
    dot_general x13 -> x9, matrix products: 11.6 us -> 4.7 us  [token_sum(): lax.dot_general(left, right, (((0,), (0,)), ((), ())), preferred_element_...]
    pallas_call x3, Pallas kernels: 138 us -> 131 us  [call(): pl.pallas_call(kernel, out_shape=[jax.ShapeDtypeStruct(s, d) for s, d in...]
    concatenate x2 -> x0, local copies, waits for them, and re-layouts: 3.46 us -> none  [row_stacked(): jnp.concatenate([rounded(left), rounded(right)], axis=1)]
    dot_general x11 -> x12, matrix products: 11.1 us -> 13.8 us  [product(): return jnp.dot(left, right, preferred_element_type=jnp.float32)]
    add x1 -> x0, other arithmetic: 2.23 us -> none  [body(): both = adjoint + summed]
    dot_general x13 -> x10, matrix products: 13.5 us -> 11.6 us  [times_transpose(): lax.dot_general(left, right, (((1,), (1,)), ((), ())), preferred_element_...]
    unnamed x85 -> x72, local copies, waits for them, and re-layouts: 9.76 us -> 11 us
where the time goes in v3:
time: 178 us; the launch traced here: 177 us
  Pallas kernels  131 us (74%)
  matrix products  30.1 us (17%)
  local copies, waits for them, and re-layouts  11.7 us (7%)
  other arithmetic  2.88 us (2%)
    pallas_call x3, Pallas kernels, call(): pl.pallas_call(kernel, out_shape=[jax.ShapeDtypeStruct(s, d) for s, d in...  131 us
    dot_general x12, matrix products, product(): return jnp.dot(left, right, preferred_element_type=jnp.float32)  13.8 us
    dot_general x10, matrix products, times_transpose(): lax.dot_general(left, right, (((1,), (1,)), ((), ())), preferred_element_...  11.6 us
    unnamed x72, local copies, waits for them, and re-layouts  11 us
    dot_general x9, matrix products, token_sum(): lax.dot_general(left, right, (((0,), (0,)), ((), ())), preferred_element_...  4.7 us

profile of v3, /device:TPU:0, one launch (start us, length us, event | category | flops | bytes accessed | tf_op | source)
XLA Modules:
  0.0 177.3 jit_solution(4231504702223923469)
XLA Ops:
  0.7 2.2 %convolution_convert_fusion.4 = bf16[1024,256]{1,0:T(8,128)(2,1)S(1)} fusion(bf16[1024,768]{1,0:T(8,128)(2,1)} %inputs.3, bf16[768,256]{1,0:T(8,128)(2,1)} %proj_key.1), kind=kOutput, calls=%fused_computation.34 | convolution fusion | flops 402915328 | bytes 2490368 | tf_op jit(solution)/shard_map/dot_general | solution.py:26
  3.5 1.4 convolution_convert_fusion.3
  4.9 1.4 convolution_convert_fusion.2
  6.8 0.6 copy-done.4
  7.8 1.0 copy-done.9
  8.8 2.6 %multiply_convert_fusion.5 = (bf16[1024,512]{1,0:T(8,128)(2,1)S(1)}, bf16[1024,512]{1,0:T(8,128)(2,1)S(1)}, bf16[1024,512]{1,0:T(8,128)(2,1)S(1)}, f32[1024,512]{1,0:T(8,128)}) fusion(f32[1024,512]{1,0:T(8,128)S(1)} %fusion.28, f32[1024,512]{1,0:T(8,128)S(1)} %fusion.25, f32[512,256]{1,0:T(8,128)S(1)} %copy-done.9, ...), kind=kOutput, calls=%fused_computation.18 | convolution fusion | flops 277217280 | bytes 10489856 | tf_op jit(solution)/shard_map/dot_general | solution.py:36
  11.8 0.8 convolution_convert_fusion.11
  13.1 1.0 pad_maximum_fusion
  14.1 42.9 %shard_map.169 = (bf16[256,512]{1,0:T(8,128)(2,1)}, bf16[256,512]{1,0:T(8,128)(2,1)}, bf16[512,256]{1,0:T(8,128)(2,1)}, f32[768,512]{1,0:T(8,128)}) custom-call(bf16[8,96,512]{2,1,0:T(8,128)(2,1)} %bitcast.53, f32[256,512]{1,0:T(8,128)} %fast_in.1, f32[256,512]{1,0:T(8,128)} %fast_up.1, f32[512,256]{1,0:T(8,128)} %fast_out.1), custom_call_target="tpu_custom_call" | custom-call | tf_op jit(solution)/shard_map/pallas_call | solution.py:380
  57.0 1.6 fusion.37
  59.6 1.4 multiply_convert_fusion.2
  62.4 1.3 fusion.9.query_grad
  64.1 1.0 pad_maximum_fusion.1
  65.1 1.2 convolution_convert_fusion.output_rows
  66.3 53.1 %shard_map.170 = (f32[768,512]{1,0:T(8,128)}, bf16[768,512]{1,0:T(8,128)(2,1)}, f32[96,512]{1,0:T(8,128)}) custom-call(bf16[8,96,512]{2,1,0:T(8,128)(2,1)} %bitcast.52, bf16[1024,768]{1,0:T(8,128)(2,1)} %inputs.3, bf16[1024,256]{1,0:T(8,128)(2,1)} %fusion.9.query_grad, bf16[1024,768]{1,0:T(8,128)(2,1)} %cotangent.1, ...), custom_call_target="tpu_custom_call" | custom-call | tf_op jit(solution)/shard_map/pallas_call | solution.py:380
  119.4 1.5 fusion.20
  121.5 0.7 copy-done.13
  122.7 0.7 slice_bitcast_fusion
  124.3 0.7 copy-done.32
  125.0 0.7 copy-done.8
  125.8 3.1 %fusion.6 = (bf16[1024,512]{1,0:T(8,128)(2,1)S(1)}, bf16[1024,512]{1,0:T(8,128)(2,1)S(1)}, bf16[1024,512]{1,0:T(8,128)(2,1)S(1)}) fusion(f32[1024,512]{1,0:T(8,128)S(1)} %fusion.28, f32[1024,512]{1,0:T(8,128)S(1)} %fusion.18, f32[1024,512]{1,0:T(8,128)S(1)} %copy-done.32, f32[1024,512]{1,0:T(8,128)S(1)} %copy-done.8, f32[1024,512]{1,0:T(8,128)S(1)} %fusion.22, ...), kind=kOutput, calls=%fused_computation.8 | convolution fusion | flops 286523392 | bytes 14422016 | tf_op jit(solution)/shard_map/dot_general | solution.py:26
  128.9 1.8 %fusion.12 = (f32[1024]{0:T(1024)}, bf16[1024,256]{1,0:T(8,128)(2,1)}) fusion(bf16[1024,256]{1,0:T(8,128)(2,1)S(1)} %copy-done.19, f32[1024]{0:T(1024)S(1)} %copy-done.31, f32[1024,256]{1,0:T(8,128)S(1)} %fusion.13, bf16[1024,512]{1,0:T(8,128)(2,1)S(1)} %get-tuple-element.36, f32[512,256]{1,0:T(8,128)S(1)} %copy-done.10), kind=kOutput, calls=%fused_computation.45 | convolution fusion | flops 270138368 | bytes 3678208 | tf_op jit(solution)/shard_map/dot_general | solution.py:26
  130.8 0.8 convolution_convert_fusion.5
  132.6 1.3 fusion.10.key_grad
  134.3 0.9 pad_maximum_fusion.2
  135.2 35.5 %shard_map.171 = (f32[256,512]{1,0:T(8,128)}, f32[256,512]{1,0:T(8,128)}, f32[512,256]{1,0:T(8,128)}, f32[96,256]{1,0:T(8,128)}, f32[96,256]{1,0:T(8,128)}, /*index=5*/bf16[1024,768]{1,0:T(8,128)(2,1)}) custom-call(bf16[8,96,512]{2,1,0:T(8,128)(2,1)} %bitcast.51, bf16[1024,768]{1,0:T(8,128)(2,1)} %inputs.3, bf16[1024,256]{1,0:T(8,128)(2,1)} %fusion.9.query_grad, ...), custom_call_target="tpu_custom_call" | custom-call | tf_op jit(solution)/shard_map/pallas_call | solution.py:380
  170.8 2.8 %copy.31 = bf16[1024,768]{1,0:T(8,128)(2,1)} copy(bf16[1024,768]{1,0:T(8,128)(2,1)} %get-tuple-element.58) | data formatting | bytes 3145728
  173.6 0.8 copy.32
  174.4 0.8 copy.33
  175.2 0.8 copy.34
  176.0 0.6 copy.35
  176.6 0.6 copy.36
  (78 shorter events, 8.6 us)
Async XLA Ops:
  0.6 4.3 %copy-start = (bf16[256,768]{1,0:T(8,128)(2,1)S(1)}, bf16[256,768]{1,0:T(8,128)(2,1)}, u32[]{:S(2)}) copy-start(bf16[256,768]{1,0:T(8,128)(2,1)} %param.15) | copy-start | bytes 1179652
  0.7 2.2 %copy-start.1 = (bf16[1024,768]{1,0:T(8,128)(2,1)S(1)}, bf16[1024,768]{1,0:T(8,128)(2,1)}, u32[]{:S(2)}) copy-start(bf16[1024,768]{1,0:T(8,128)(2,1)} %inputs.3) | copy-start | bytes 4718596
  0.7 2.2 %copy-start.25 = (bf16[768,256]{1,0:T(8,128)(2,1)S(1)}, bf16[768,256]{1,0:T(8,128)(2,1)}, u32[]{:S(2)}) copy-start(bf16[768,256]{1,0:T(8,128)(2,1)} %proj_value.1) | copy-start | bytes 1179652
  0.7 2.8 %copy-start.26 = (bf16[768,256]{1,0:T(8,128)(2,1)S(1)}, bf16[768,256]{1,0:T(8,128)(2,1)}, u32[]{:S(2)}) copy-start(bf16[768,256]{1,0:T(8,128)(2,1)} %proj_query.1) | copy-start | bytes 1179652
  2.9 2.0 %copy-start.11 = (bf16[1024,768]{1,0:T(8,128)(2,1)S(1)}, bf16[1024,768]{1,0:T(8,128)(2,1)}, u32[]{:S(2)}) copy-start(bf16[1024,768]{1,0:T(8,128)(2,1)} %cotangent.1) | copy-start | bytes 4718596
  3.5 8.3 %copy-start.18 = (bf16[1024,256]{1,0:T(8,128)(2,1)}, bf16[1024,256]{1,0:T(8,128)(2,1)S(1)}, u32[]{:S(2)}) copy-start(bf16[1024,256]{1,0:T(8,128)(2,1)S(1)} %convolution_convert_fusion.1) | copy-start | bytes 1572868
  3.5 2.8 %copy-start.2 = (f32[256,512]{1,0:T(8,128)S(1)}, f32[256,512]{1,0:T(8,128)}, u32[]{:S(2)}) copy-start(f32[256,512]{1,0:T(8,128)} %fast_in.1) | copy-start | bytes 1572868
  6.3 1.0 copy-start.4
  7.4 4.0 %copy-start.7 = (f32[1024,512]{1,0:T(8,128)}, f32[1024,512]{1,0:T(8,128)S(1)}, u32[]{:S(2)}) copy-start(f32[1024,512]{1,0:T(8,128)S(1)} %fusion.25) | copy-start | bytes 6291460
  7.4 1.4 copy-start.9
  7.4 1.4 copy-start.31
  11.4 1.3 copy-start.12
  11.4 1.3 copy-start.14
  57.0 1.7 copy-start.17
  57.0 1.7 copy-start.23
  59.6 1.4 copy-start.24
  63.6 1.4 copy-start.16
  119.4 1.6 copy-start.6
  119.4 1.6 copy-start.15
  121.0 1.2 copy-start.13
  121.0 1.7 copy-start.28
  123.4 1.6 copy-start.32
  123.8 1.9 %copy-start.8 = (f32[1024,512]{1,0:T(8,128)S(1)}, f32[1024,512]{1,0:T(8,128)}, u32[]{:S(2)}) copy-start(f32[1024,512]{1,0:T(8,128)} %copy-done.7) | copy-start | bytes 6291460
  123.8 2.0 %copy-start.19 = (bf16[1024,256]{1,0:T(8,128)(2,1)S(1)}, bf16[1024,256]{1,0:T(8,128)(2,1)}, u32[]{:S(2)}) copy-start(bf16[1024,256]{1,0:T(8,128)(2,1)} %copy-done.18) | copy-start | bytes 1572868
  125.8 3.1 %copy-start.10 = (f32[512,256]{1,0:T(8,128)S(1)}, f32[512,256]{1,0:T(8,128)}, u32[]{:S(2)}) copy-start(f32[512,256]{1,0:T(8,128)} %fast_out.1) | copy-start | bytes 1572868
  128.9 2.6 %copy-start.3 = (f32[256,512]{1,0:T(8,128)S(1)}, f32[256,512]{1,0:T(8,128)}, u32[]{:S(2)}) copy-start(f32[256,512]{1,0:T(8,128)} %fast_in.1) | copy-start | bytes 1572868
  131.5 1.0 copy-start.5
  170.8 2.8 %copy-start.22 = (f32[256,512]{1,0:T(8,128)S(1)}, f32[256,512]{1,0:T(8,128)}, u32[]{:S(2)}) copy-start(f32[256,512]{1,0:T(8,128)} %get-tuple-element.60) | copy-start | bytes 1572868
  170.8 3.6 %copy-start.21 = (f32[256,512]{1,0:T(8,128)S(1)}, f32[256,512]{1,0:T(8,128)}, u32[]{:S(2)}) copy-start(f32[256,512]{1,0:T(8,128)} %get-tuple-element.61) | copy-start | bytes 1572868
  170.8 4.4 %copy-start.20 = (f32[512,256]{1,0:T(8,128)S(1)}, f32[512,256]{1,0:T(8,128)}, u32[]{:S(2)}) copy-start(f32[512,256]{1,0:T(8,128)} %get-tuple-element.62) | copy-start | bytes 1572868
  173.6 2.4 %copy-start.30 = (f32[96,256]{1,0:T(8,128)S(1)}, f32[96,256]{1,0:T(8,128)}, u32[]{:S(2)}) copy-start(f32[96,256]{1,0:T(8,128)} %get-tuple-element.64) | copy-start | bytes 294916
  173.6 3.0 %copy-start.29 = (f32[96,256]{1,0:T(8,128)S(1)}, f32[96,256]{1,0:T(8,128)}, u32[]{:S(2)}) copy-start(f32[96,256]{1,0:T(8,128)} %get-tuple-element.65) | copy-start | bytes 294916
  (1 other events, 1.0 us)

commit v4 on v3

--- a/solution.py
+++ b/solution.py
@@ -176,10 +176,11 @@
     return copies
 
 
-def forward_pairs(lines, src, buf, copies):
+def forward_pairs(lines, src, buf, copies, first=1, last=None):
     line, side = place()
     sent = []
-    for d, copy in zip(range(1, lines), copies):
+    for d in range(lines if last is None else last)[first:]:
+        copy = copies[d - 1]
         to = lax.rem(line + d, lines)
         copy.wait()
         buf.middle[d] = rounded(
@@ -276,11 +277,14 @@
 
 
 def forward_kernel(
-    lines, count, part, fast_in, fast_up, fast_out, n_in, n_up, n_out, total_out, *scratch
+    lines, count, part, fast_in, fast_up, fast_out, inputs, proj_query, cotangent, proj_output,
+    n_in, n_up, n_out, total_out, query_rows, back_output, *scratch
 ):
     buf, xs = Reduce(*scratch[:7]), scratch[7]
     greet(lines)
     copies = start_pairs(lines, part, buf)
+    query_rows[...] = rounded(product(inputs[...], proj_query[...]))
+    back_output[...] = rounded(times_transpose(cotangent[...], proj_output[...]))
     sent = forward_pairs(lines, part, buf, copies)
     buf.mine[...] = rounded(finish_scatter(lines, part, buf, copies, sent))
     gathering = start_gather(lines, buf)
@@ -318,13 +322,15 @@
     totals = [total_ref[m * h : (m + 1) * h, :] for m in range(count)]
     norms = ns_start(totals, xs)
     fill_rows(rows_part, ((inputs, query_grad), (cotangent, output_rows)))
+    sent = forward_pairs(lines, part, buf, copies, 1, lines - 1)
     ns_forward(0, NS_STEPS - 4, xs, grams, polys, count, PASSES_FWD)
-    sent = forward_pairs(lines, part, buf, copies)
+    sent += forward_pairs(lines, part, buf, copies, lines - 1)
     ns_forward(NS_STEPS - 4, NS_STEPS - 2, xs, grams, polys, count, PASSES_FWD)
     buf.mine[...] = rounded(finish_scatter(lines, part, buf, copies, sent))
     gathering = start_gather(lines, buf)
-    ns_forward(NS_STEPS - 2, NS_STEPS, xs, grams, polys, count, PASSES_FWD)
+    ns_forward(NS_STEPS - 2, NS_STEPS - 1, xs, grams, polys, count, PASSES_FWD)
     relay_gather(lines, buf, gathering)
+    ns_forward(NS_STEPS - 1, NS_STEPS, xs, grams, polys, count, PASSES_FWD)
     finish_gather(lines, buf, gathering, adjoint_out)
     copies = start_pairs(lines, rows_part, row_buf)
     for m in range(count):
@@ -409,7 +415,6 @@
     block = (count * h // n, f)
     row_block = (width // n, 2 * h)
 
-    query_rows = rounded(product(inputs, proj_query))
     key_rows = rounded(product(inputs, proj_key))
     value_rows = rounded(product(inputs, proj_value))
     w_in, w_up, w_out = (rounded(fast_in), rounded(fast_up), rounded(fast_out))
@@ -433,12 +438,19 @@
     lines = n // PAIR
     exchange = Reduce.scratch(lines, block)
     row_scratch = Scatter.scratch(lines, row_block)
-    n_in, n_up, n_out, totals = call(
+    n_in, n_up, n_out, totals, query_rows, back_output = call(
         functools.partial(forward_kernel, lines, count),
         0,
-        [((h, f), bf16), ((h, f), bf16), ((f, h), bf16), ((count * h, f), f32)],
+        [
+            ((h, f), bf16),
+            ((h, f), bf16),
+            ((f, h), bf16),
+            ((count * h, f), f32),
+            ((inputs.shape[0], h), bf16),
+            ((inputs.shape[0], h), bf16),
+        ],
         exchange + [pltpu.VMEM((NS_STEPS + 1, count, h, f), f32)],
-        part, fast_in, fast_up, fast_out,
+        part, fast_in, fast_up, fast_out, inputs, proj_query, cotangent, proj_output,
     )
 
     pre_p = product(query_rows, n_in)
@@ -446,7 +458,6 @@
     activation_q, slope_q, _ = silu_parts(pre_p)
     hidden_q = rounded(activation_q * pre_r)
     output_rows = rounded(product(hidden_q, n_out))
-    back_output = rounded(times_transpose(cotangent, proj_output))
     back_hidden = times_transpose(back_output, n_out)
     back_p = rounded(back_hidden * pre_r * slope_q)
     back_r = rounded(back_hidden * activation_q)

time: 178 us -> 174 us (0.978)
  matrix products: 30.1 us -> 27.1 us
    dot_general x12 -> x11, matrix products: 13.8 us -> 12.2 us  [product(): return jnp.dot(left, right, preferred_element_type=jnp.float32)]
    dot_general x10 -> x9, matrix products: 11.6 us -> 10.2 us  [times_transpose(): lax.dot_general(left, right, (((1,), (1,)), ((), ())), preferred_element_...]
    unnamed x72 -> x66, local copies, waits for them, and re-layouts: 11 us -> 10.2 us
where the time goes in v4:
time: 174 us
  Pallas kernels  132 us (76%)
  matrix products  27.1 us (16%)
  local copies, waits for them, and re-layouts  10.9 us (6%)
  other arithmetic  2.79 us (2%)
    pallas_call x3, Pallas kernels, call(): pl.pallas_call(kernel, out_shape=[jax.ShapeDtypeStruct(s, d) for s, d in...  132 us
    dot_general x11, matrix products, product(): return jnp.dot(left, right, preferred_element_type=jnp.float32)  12.2 us
    unnamed x66, local copies, waits for them, and re-layouts  10.2 us
    dot_general x9, matrix products, times_transpose(): lax.dot_general(left, right, (((1,), (1,)), ((), ())), preferred_element_...  10.2 us
    dot_general x9, matrix products, token_sum(): lax.dot_general(left, right, (((0,), (0,)), ((), ())), preferred_element_...  4.71 us

profile of v4, /device:TPU:0, one launch (start us, length us, event | category | flops | bytes accessed | tf_op | source)
XLA Modules:
  0.0 174.1 jit_solution(8901212197997865078)
XLA Ops:
  0.7 2.2 %convolution_convert_fusion.2 = bf16[1024,256]{1,0:T(8,128)(2,1)S(1)} fusion(bf16[1024,768]{1,0:T(8,128)(2,1)} %inputs.5, bf16[768,256]{1,0:T(8,128)(2,1)} %proj_key.1), kind=kOutput, calls=%fused_computation.32 | convolution fusion | flops 402915328 | bytes 2490368 | tf_op jit(solution)/shard_map/dot_general | solution.py:26
  2.9 0.6 convolution_convert_fusion.1
  3.9 0.6 copy-done.3
  5.0 1.0 copy-done.6
  5.9 2.6 %multiply_convert_fusion.5 = (bf16[1024,512]{1,0:T(8,128)(2,1)S(1)}, bf16[1024,512]{1,0:T(8,128)(2,1)S(1)}, bf16[1024,512]{1,0:T(8,128)(2,1)S(1)}, f32[1024,512]{1,0:T(8,128)}) fusion(f32[1024,512]{1,0:T(8,128)S(1)} %fusion.28, f32[1024,512]{1,0:T(8,128)S(1)} %fusion.25, f32[512,256]{1,0:T(8,128)S(1)} %copy-done.6, ...), kind=kOutput, calls=%fused_computation.18 | convolution fusion | flops 277217280 | bytes 10489856 | tf_op jit(solution)/shard_map/dot_general | solution.py:36
  9.0 0.8 convolution_convert_fusion.9
  10.3 0.9 pad_maximum_fusion
  11.3 44.1 %shard_map.169 = (bf16[256,512]{1,0:T(8,128)(2,1)}, bf16[256,512]{1,0:T(8,128)(2,1)}, bf16[512,256]{1,0:T(8,128)(2,1)}, f32[768,512]{1,0:T(8,128)}, bf16[1024,25...) custom-call(bf16[8,96,512]{2,1,0:T(8,128)(2,1)} %bitcast.49, f32[256,512]{1,0:T(8,128)} %fast_in.1, f32[256,512]{1,0:T(8,128)} %fast_up.1, ...), custom_call_target="tpu_custom_call" | custom-call | tf_op jit(solution)/shard_map/pallas_call | solution.py:386
  55.3 1.6 fusion.37
  57.4 0.5 copy-done.24
  58.0 1.4 multiply_convert_fusion.2
  60.7 1.3 fusion.9.query_grad
  62.4 0.9 pad_maximum_fusion.1
  63.4 1.2 convolution_convert_fusion.output_rows
  64.6 53.6 %shard_map.170 = (f32[768,512]{1,0:T(8,128)}, bf16[768,512]{1,0:T(8,128)(2,1)}, f32[96,512]{1,0:T(8,128)}) custom-call(bf16[8,96,512]{2,1,0:T(8,128)(2,1)} %bitcast.48, bf16[1024,768]{1,0:T(8,128)(2,1)} %inputs.5, bf16[1024,256]{1,0:T(8,128)(2,1)} %fusion.9.query_grad, bf16[1024,768]{1,0:T(8,128)(2,1)} %cotangent.3, ...), custom_call_target="tpu_custom_call" | custom-call | tf_op jit(solution)/shard_map/pallas_call | solution.py:386
  118.3 1.5 fusion.20
  120.8 0.7 slice_bitcast_fusion
  122.4 0.8 copy-done.11
  123.2 0.6 copy-done.9
  123.8 2.8 %fusion.6 = (bf16[1024,512]{1,0:T(8,128)(2,1)S(1)}, bf16[1024,512]{1,0:T(8,128)(2,1)S(1)}, bf16[1024,512]{1,0:T(8,128)(2,1)S(1)}) fusion(f32[1024,512]{1,0:T(8,128)S(1)} %copy-done.11, f32[1024,512]{1,0:T(8,128)S(1)} %fusion.18, f32[1024,512]{1,0:T(8,128)S(1)} %copy-done.29, f32[1024,512]{1,0:T(8,128)S(1)} %copy-done.9, f32[1024,512]{1,0:T(8,128)S(1)} %fusion.22, ...), kind=kOutput, calls=%fused_computation.8 | convolution fusion | flops 286523392 | bytes 14422016 | tf_op jit(solution)/shard_map/dot_general | solution.py:26
  126.7 1.8 %fusion.12 = (f32[1024]{0:T(1024)}, bf16[1024,256]{1,0:T(8,128)(2,1)}) fusion(bf16[1024,256]{1,0:T(8,128)(2,1)S(1)} %convolution_convert_fusion.1, f32[1024]{0:T(1024)S(1)} %copy-done.28, f32[1024,256]{1,0:T(8,128)S(1)} %fusion.13, bf16[1024,512]{1,0:T(8,128)(2,1)S(1)} %get-tuple-element.40, f32[512,256]{1,0:T(8,128)S(1)} %copy-done.7), kind=kOutput, calls=%fused_computation.43 | convolution fusion | flops 270138368 | bytes 3678208 | tf_op jit(solution)/shard_map/dot_general | solution.py:26
  128.5 0.8 convolution_convert_fusion.3
  129.3 0.5 convolution_add_fusion.2
  130.4 1.3 fusion.10.key_grad
  132.1 0.9 pad_maximum_fusion.2
  133.0 34.6 %shard_map.171 = (f32[256,512]{1,0:T(8,128)}, f32[256,512]{1,0:T(8,128)}, f32[512,256]{1,0:T(8,128)}, f32[96,256]{1,0:T(8,128)}, f32[96,256]{1,0:T(8,128)}, /*index=5*/bf16[1024,768]{1,0:T(8,128)(2,1)}) custom-call(bf16[8,96,512]{2,1,0:T(8,128)(2,1)} %bitcast.47, bf16[1024,768]{1,0:T(8,128)(2,1)} %inputs.5, bf16[1024,256]{1,0:T(8,128)(2,1)} %fusion.9.query_grad, ...), custom_call_target="tpu_custom_call" | custom-call | tf_op jit(solution)/shard_map/pallas_call | solution.py:386
  167.7 2.8 %copy.31 = bf16[1024,768]{1,0:T(8,128)(2,1)} copy(bf16[1024,768]{1,0:T(8,128)(2,1)} %get-tuple-element.62) | data formatting | bytes 3145728
  170.4 0.8 copy.32
  171.2 0.8 copy.33
  172.0 0.8 copy.34
  172.8 0.6 copy.35
  173.5 0.6 copy.36
  (70 shorter events, 7.0 us)
Async XLA Ops:
  0.6 2.2 %copy-start = (bf16[1024,768]{1,0:T(8,128)(2,1)S(1)}, bf16[1024,768]{1,0:T(8,128)(2,1)}, u32[]{:S(2)}) copy-start(bf16[1024,768]{1,0:T(8,128)(2,1)} %inputs.5) | copy-start | bytes 4718596
  0.7 2.8 %copy-start.1 = (f32[256,512]{1,0:T(8,128)S(1)}, f32[256,512]{1,0:T(8,128)}, u32[]{:S(2)}) copy-start(f32[256,512]{1,0:T(8,128)} %fast_in.1) | copy-start | bytes 1572868
  0.7 2.2 %copy-start.23 = (bf16[768,256]{1,0:T(8,128)(2,1)S(1)}, bf16[768,256]{1,0:T(8,128)(2,1)}, u32[]{:S(2)}) copy-start(bf16[768,256]{1,0:T(8,128)(2,1)} %proj_value.1) | copy-start | bytes 1179652
  3.5 1.0 copy-start.3
  4.5 4.0 %copy-start.8 = (f32[1024,512]{1,0:T(8,128)}, f32[1024,512]{1,0:T(8,128)S(1)}, u32[]{:S(2)}) copy-start(f32[1024,512]{1,0:T(8,128)S(1)} %fusion.25) | copy-start | bytes 6291460
  4.5 1.4 copy-start.6
  4.5 1.4 copy-start.28
  5.9 2.6 %copy-start.10 = (f32[1024,512]{1,0:T(8,128)}, f32[1024,512]{1,0:T(8,128)S(1)}, u32[]{:S(2)}) copy-start(f32[1024,512]{1,0:T(8,128)S(1)} %fusion.28) | copy-start | bytes 6291460
  8.5 1.3 copy-start.12
  8.6 1.3 copy-start.14
  55.3 1.7 copy-start.17
  55.3 1.7 copy-start.21
  57.0 1.0 copy-start.24
  57.9 1.4 copy-start.22
  62.0 1.4 copy-start.16
  64.6 53.7 %copy-start.15 = (bf16[1024,512]{1,0:T(8,128)(2,1)S(1)}, bf16[1024,512]{1,0:T(8,128)(2,1)}, u32[]{:S(2)}) copy-start(bf16[1024,512]{1,0:T(8,128)(2,1)} %copy-done.14) | copy-start | bytes 3145732
  118.2 1.6 copy-start.5
  118.3 1.6 copy-start.13
  119.8 1.0 copy-start.25
  120.3 2.1 %copy-start.29 = (f32[1024,512]{1,0:T(8,128)S(1)}, f32[1024,512]{1,0:T(8,128)}, u32[]{:S(2)}) copy-start(f32[1024,512]{1,0:T(8,128)} %get-tuple-element.52) | copy-start | bytes 6291460
  121.5 1.7 copy-start.11
  121.9 1.9 %copy-start.9 = (f32[1024,512]{1,0:T(8,128)S(1)}, f32[1024,512]{1,0:T(8,128)}, u32[]{:S(2)}) copy-start(f32[1024,512]{1,0:T(8,128)} %copy-done.8) | copy-start | bytes 6291460
  123.8 2.9 %copy-start.7 = (f32[512,256]{1,0:T(8,128)S(1)}, f32[512,256]{1,0:T(8,128)}, u32[]{:S(2)}) copy-start(f32[512,256]{1,0:T(8,128)} %fast_out.1) | copy-start | bytes 1572868
  126.7 2.6 %copy-start.2 = (f32[256,512]{1,0:T(8,128)S(1)}, f32[256,512]{1,0:T(8,128)}, u32[]{:S(2)}) copy-start(f32[256,512]{1,0:T(8,128)} %fast_in.1) | copy-start | bytes 1572868
  129.3 1.0 copy-start.4
  167.6 2.8 %copy-start.20 = (f32[256,512]{1,0:T(8,128)S(1)}, f32[256,512]{1,0:T(8,128)}, u32[]{:S(2)}) copy-start(f32[256,512]{1,0:T(8,128)} %get-tuple-element.64) | copy-start | bytes 1572868
  167.6 3.6 %copy-start.19 = (f32[256,512]{1,0:T(8,128)S(1)}, f32[256,512]{1,0:T(8,128)}, u32[]{:S(2)}) copy-start(f32[256,512]{1,0:T(8,128)} %get-tuple-element.65) | copy-start | bytes 1572868
  167.6 4.4 %copy-start.18 = (f32[512,256]{1,0:T(8,128)S(1)}, f32[512,256]{1,0:T(8,128)}, u32[]{:S(2)}) copy-start(f32[512,256]{1,0:T(8,128)} %get-tuple-element.66) | copy-start | bytes 1572868
  170.4 2.4 %copy-start.27 = (f32[96,256]{1,0:T(8,128)S(1)}, f32[96,256]{1,0:T(8,128)}, u32[]{:S(2)}) copy-start(f32[96,256]{1,0:T(8,128)} %get-tuple-element.68) | copy-start | bytes 294916
  170.4 3.0 %copy-start.26 = (f32[96,256]{1,0:T(8,128)S(1)}, f32[96,256]{1,0:T(8,128)}, u32[]{:S(2)}) copy-start(f32[96,256]{1,0:T(8,128)} %get-tuple-element.69) | copy-start | bytes 294916
